TPU v7x, 32 devices: a whole 2x2x4 slice. The times are simulated.
32 devices in a mesh: ctx: 16 (over z, y, core), shard: 2 (over x).
Axes of the slice: x: 2, y: 2, z: 4, core: 2. Of those that a mesh axis runs over, the one named last changes fastest.
Arguments:
- tokens: bfloat16 [2, 8192, 1024], P('shard', 'ctx'), may hold values from -6 to 6
- teacher: bfloat16 [2, 8192, 1024], P('shard', 'ctx'), may hold values from -6 to 6
- cotangent: bfloat16 [2, 8192, 1024], P('shard', 'ctx'), may hold values from -6 to 6
- doc_starts: int32 [2, 18], P('shard'), may hold values from 0 to 8192, as said below
- doc_time: int32 [2, 18], P('shard'), may hold values from 0 to 999
- valid_mask: int32 [2, 8192], P('shard', 'ctx'), may hold values from 0 to 1, as said below
- gain_one: bfloat16 [1024], P('shard'), may hold values from 0.5 to 1.5
- bias_one: bfloat16 [1024], P('shard'), may hold values from -4 to 4
- time_one: bfloat16 [256, 1024], P('shard'), may hold values from -0.375 to 0.375
- qkv_weight: bfloat16 [1024, 3072], P('shard'), may hold values from -0.1875 to 0.1875
- out_weight: bfloat16 [1024, 1024], P('shard'), may hold values from -1.5 to 1.5
- gain_two: bfloat16 [1024], P('shard'), may hold values from 0.5 to 1.5
- bias_two: bfloat16 [1024], P('shard'), may hold values from -4 to 4
- time_two: bfloat16 [256, 1024], P('shard'), may hold values from -0.375 to 0.375
- up_weight: bfloat16 [1024, 4096], P('shard'), may hold values from -0.1875 to 0.1875
- up_bias: bfloat16 [4096], P('shard'), may hold values from -4 to 4
- down_weight: bfloat16 [4096, 1024], P('shard'), may hold values from -0.09375 to 0.09375
- down_bias: bfloat16 [1024], P('shard'), may hold values from -4 to 4
Outputs:
- output: bfloat16 [2, 8192, 1024], P('shard', 'ctx')
- loss_value: float32 [], replicated
- input_grad: float32 [2, 8192, 1024], P('shard', 'ctx')
- grad_gain_one: float32 [1024], P('shard')
- grad_bias_one: float32 [1024], P('shard')
- grad_time_one: float32 [256, 1024], P('shard')
- grad_qkv_weight: float32 [1024, 3072], P('shard')
- grad_out_weight: float32 [1024, 1024], P('shard')
- grad_gain_two: float32 [1024], P('shard')
- grad_bias_two: float32 [1024], P('shard')
- grad_time_two: float32 [256, 1024], P('shard')
- grad_up_weight: float32 [1024, 4096], P('shard')
- grad_up_bias: float32 [4096], P('shard')
- grad_down_weight: float32 [4096, 1024], P('shard')
- grad_down_bias: float32 [1024], P('shard')
Inputs may be any that keep to these rules, and one draw needn't show every extreme that they name: `doc_starts`: each pack's row begins with 0 and never falls; every entry below 8192 opens a document that runs to the next larger entry (or to 8192) and has 1 to 2048 tokens; every pack has a document of exactly 2048 tokens; slots past the pack's end, the last slot among them, hold 8192. `valid_mask`: the last token of every pack has 1.
All inputs are finite; a program needn't handle non-finite values.
Results may differ from a plain program's by a relative error of at most 0.024.
Values may be sent and summed in bfloat16 or wider, within the bound.
No kernel may reach another device: no remote copies, remote signals or barrier semaphores. Data moves between devices by JAX's collectives and lax.ppermute only.
A program may use at most 320 MiB of HBM per device.

v0:
```python
from functools import partial
import math

import jax
import jax.numpy as jnp
from jax import lax
from jax.sharding import PartitionSpec as P

HEADS = 16
HEAD = 64
TEMB = 256
REACH = 4


norm_eps = 1e-05
masked_value = -1e30


def from_behind(x, axis, by):
    size = lax.axis_size(axis)
    pairs = [(i, i + by) for i in range(size) if 0 <= i + by < size]
    return lax.ppermute(x, axis, pairs)


def doc_fields(starts, stamps, places):
    inside = starts[None, :] <= places[:, None]
    segment = jnp.sum(inside.astype(jnp.int32), axis=1) - 1
    doc_begin = jnp.max(jnp.where(inside, starts[None, :], 0), axis=1)
    slot_ids = jnp.arange(starts.shape[0], dtype=jnp.int32)
    time_index = jnp.sum(
        jnp.where(segment[:, None] == slot_ids[None, :], stamps[None, :], 0), axis=1
    )
    return (segment, places - doc_begin, time_index)


def time_features(time_index):
    halfway = TEMB // 2
    ladder = jnp.exp(-math.log(10000.0) * jnp.arange(halfway, dtype=jnp.float32) / halfway)
    phases = time_index.astype(jnp.float32)[:, None] * ladder[None, :]
    return jnp.concatenate([jnp.sin(phases), jnp.cos(phases)], axis=1)


def rotate(vectors, places):
    count_rows = vectors.shape[0]
    halfway = HEAD // 2
    ladder = jnp.exp(-math.log(10000.0) * 2.0 * jnp.arange(halfway, dtype=jnp.float32) / HEAD)
    turned = places.astype(jnp.float32)[:, None] * ladder[None, :]
    cosine = jnp.cos(turned)[:, None, :]
    sine_part = jnp.sin(turned)[:, None, :]
    split_heads = vectors.reshape(count_rows, HEADS, HEAD)
    former = split_heads[:, :, :halfway]
    latter = split_heads[:, :, halfway:]
    joined = jnp.concatenate(
        [former * cosine - latter * sine_part, former * sine_part + latter * cosine], axis=2
    )
    return joined.reshape(count_rows, HEADS * HEAD)


def inner_rows(left_side, right_side):
    return lax.dot_general(
        left_side, right_side, (((0,), (0,)), ((), ())), preferred_element_type=jnp.float32
    )


def times_trans(left_side, right_side):
    return lax.dot_general(
        left_side, right_side, (((1,), (1,)), ((), ())), preferred_element_type=jnp.float32
    )


def norm_forward(values, gain_vec, bias_vec, features, time_weight):
    average = jnp.mean(values, axis=1, keepdims=True)
    centred = values - average
    inv_std = lax.rsqrt(jnp.mean(centred * centred, axis=1, keepdims=True) + norm_eps)
    normed = centred * inv_std
    scales = gain_vec.astype(jnp.float32)[None, :] + jnp.dot(
        features, time_weight, preferred_element_type=jnp.float32
    )
    return (normed * scales + bias_vec.astype(jnp.float32)[None, :], normed, scales, inv_std)


def norm_backward(grad_act, normed, scales, inv_std, features):
    grad_scale = grad_act * normed
    grad_gain = jnp.sum(grad_scale, axis=0)
    grad_bias = jnp.sum(grad_act, axis=0)
    grad_time = inner_rows(features, grad_scale.astype(jnp.bfloat16))
    grad_norm = grad_act * scales
    grad_input = inv_std * (
        grad_norm
        - jnp.mean(grad_norm, axis=1, keepdims=True)
        - normed * jnp.mean(grad_norm * normed, axis=1, keepdims=True)
    )
    return (grad_input, grad_gain, grad_bias, grad_time)


def masked_scores(query_heads, key_block, query_seg, key_seg):
    key_heads = key_block.reshape(key_block.shape[0], HEADS, HEAD)
    raw_scores = jnp.einsum(
        "qhd,khd->hqk", query_heads, key_heads, preferred_element_type=jnp.float32
    ) * HEAD ** (-0.5)
    return jnp.where((query_seg[:, None] == key_seg[None, :])[None], raw_scores, masked_value)


def score_grads(query_heads, grad_heads, log_total, row_delta, kv_pair, query_seg, key_seg):
    scores = masked_scores(query_heads, kv_pair[0], query_seg, key_seg)
    prob_full = jnp.exp(scores - log_total[:, :, None])
    value_heads = kv_pair[1].reshape(kv_pair.shape[1], HEADS, HEAD)
    grad_prob = jnp.einsum(
        "qhd,khd->hqk", grad_heads, value_heads, preferred_element_type=jnp.float32
    )
    grad_scores = (prob_full * (grad_prob - row_delta[:, :, None]) * HEAD ** (-0.5)).astype(
        jnp.bfloat16
    )
    return (prob_full.astype(jnp.bfloat16), grad_scores)


def keep_state(state_now):
    return state_now


def fetch_pair(kv_pair, shift_by):
    return from_behind(kv_pair, "ctx", shift_by)


def send_back(grad_pair, shift_by):
    return from_behind(grad_pair.astype(jnp.bfloat16), "ctx", -shift_by).astype(grad_pair.dtype)


def on_device(
    tokens,
    teacher,
    cotangent,
    doc_starts,
    doc_time,
    valid_mask,
    gain_one,
    bias_one,
    time_one,
    qkv_weight,
    out_weight,
    gain_two,
    bias_two,
    time_two,
    up_weight,
    up_bias,
    down_weight,
    down_bias,
):
    tok_rows = tokens.shape[1]
    width_d = tokens.shape[2]
    blocks_ctx = lax.axis_size("ctx")
    position = lax.axis_index("ctx")
    starts = doc_starts[0]
    stamps = doc_time[0]

    def block_segments(block_index):
        places = block_index * tok_rows + jnp.arange(tok_rows, dtype=jnp.int32)
        return doc_fields(starts, stamps, places)

    own_seg, own_place, own_time = block_segments(position)
    features = time_features(own_time).astype(jnp.bfloat16)
    block_in = tokens[0].astype(jnp.float32)
    gain_attn, bias_attn, time_attn, qkv_full, out_full = (
        lax.all_gather(gain_one, "shard", axis=0, tiled=True),
        lax.all_gather(bias_one, "shard", axis=0, tiled=True),
        lax.all_gather(time_one, "shard", axis=0, tiled=True),
        lax.all_gather(qkv_weight, "shard", axis=0, tiled=True),
        lax.all_gather(out_weight, "shard", axis=0, tiled=True),
    )
    act_pre, normed_one, scales_one, inv_one = norm_forward(
        block_in, gain_attn, bias_attn, features, time_attn
    )
    act_one = act_pre.astype(jnp.bfloat16)
    joined = jnp.dot(act_one, qkv_full, preferred_element_type=jnp.float32)
    query_low = rotate(joined[:, :width_d], own_place).astype(jnp.bfloat16)
    key_low = rotate(joined[:, width_d : 2 * width_d], own_place).astype(jnp.bfloat16)
    value_low = joined[:, 2 * width_d :].astype(jnp.bfloat16)
    query_heads = query_low.reshape(tok_rows, HEADS, HEAD)
    own_pair = jnp.stack([key_low, value_low])
    offsets = [shift_by for shift_by in range(1, REACH + 1)] + [
        -shift_by for shift_by in range(1, REACH + 1)
    ]
    pair_list = [own_pair]
    seg_list = [own_seg]
    live_list = [jnp.array(True)]
    for shift_by in offsets:
        pair_list.append(fetch_pair(own_pair, shift_by))
        key_index = position - shift_by
        key_seg = block_segments(key_index)[0]
        seg_list.append(key_seg)
        inrange = jnp.logical_and(key_index >= 0, key_index < blocks_ctx)
        live_list.append(inrange & (key_seg[0] <= own_seg[-1]) & (key_seg[-1] >= own_seg[0]))
    key_stacks = (jnp.stack(pair_list), jnp.stack(seg_list), jnp.stack(live_list))

    def attend_step(running, block_item):
        kv_pair, key_seg, is_live = block_item

        def attend_active(state_now):
            top_old, total_old, acc_old = state_now
            scores = masked_scores(query_heads, kv_pair[0], own_seg, key_seg)
            top_new = jnp.maximum(top_old, jnp.max(scores, axis=2))
            weights = jnp.exp(scores - top_new[:, :, None])
            rescale = jnp.exp(top_old - top_new)
            total_new = total_old * rescale + jnp.sum(weights, axis=2)
            value_heads = kv_pair[1].reshape(tok_rows, HEADS, HEAD)
            acc_new = acc_old * jnp.transpose(rescale)[:, :, None] + jnp.einsum(
                "hqk,khd->qhd",
                weights.astype(jnp.bfloat16),
                value_heads,
                preferred_element_type=jnp.float32,
            )
            return (top_new, total_new, acc_new)

        return (lax.cond(is_live, attend_active, keep_state, running), None)

    start_top = jnp.full((HEADS, tok_rows), masked_value, jnp.float32)
    start_sum = jnp.zeros((HEADS, tok_rows), jnp.float32)
    start_acc = jnp.zeros((tok_rows, HEADS, HEAD), jnp.float32)
    (top_all, sum_all, acc_all), unused = lax.scan(
        attend_step, (start_top, start_sum, start_acc), key_stacks
    )
    log_total = top_all + jnp.log(sum_all)
    mixed_sum = acc_all / jnp.transpose(sum_all)[:, :, None]
    mixed_low = mixed_sum.reshape(tok_rows, width_d).astype(jnp.bfloat16)
    middle = block_in + jnp.dot(mixed_low, out_full, preferred_element_type=jnp.float32)
    gain_mlp, bias_mlp, time_mlp, up_full, up_bias_full, down_full, down_bias_full = (
        lax.all_gather(gain_two, "shard", axis=0, tiled=True),
        lax.all_gather(bias_two, "shard", axis=0, tiled=True),
        lax.all_gather(time_two, "shard", axis=0, tiled=True),
        lax.all_gather(up_weight, "shard", axis=0, tiled=True),
        lax.all_gather(up_bias, "shard", axis=0, tiled=True),
        lax.all_gather(down_weight, "shard", axis=0, tiled=True),
        lax.all_gather(down_bias, "shard", axis=0, tiled=True),
    )
    act_pre_two, normed_two, scales_two, inv_two = norm_forward(
        middle, gain_mlp, bias_mlp, features, time_mlp
    )
    act_two = act_pre_two.astype(jnp.bfloat16)
    upper_in = (
        jnp.dot(act_two, up_full, preferred_element_type=jnp.float32)
        + up_bias_full.astype(jnp.float32)[None, :]
    )
    hidden = jax.nn.gelu(upper_in, approximate=False).astype(jnp.bfloat16)
    block_out = (
        middle
        + jnp.dot(hidden, down_full, preferred_element_type=jnp.float32)
        + down_bias_full.astype(jnp.float32)[None, :]
    )
    weight_mask = valid_mask[0].astype(jnp.float32)
    misfit = block_out - teacher[0].astype(jnp.float32)
    square_sum, valid_sum = lax.psum(
        (jnp.sum(weight_mask[:, None] * misfit * misfit), jnp.sum(weight_mask)), ("ctx", "shard")
    )
    loss_value = square_sum / (valid_sum * width_d)
    grad_final = (
        cotangent[0].astype(jnp.float32)
        + 2.0 / (valid_sum * width_d) * weight_mask[:, None] * misfit
    )
    grad_mid = grad_final.astype(jnp.bfloat16)
    up_back, down_back = (
        lax.all_gather(up_weight, "shard", axis=0, tiled=True),
        lax.all_gather(down_weight, "shard", axis=0, tiled=True),
    )
    grad_down = inner_rows(hidden, grad_mid)
    grad_down_bias = jnp.sum(grad_mid.astype(jnp.float32), axis=0)
    grad_hidden = times_trans(grad_mid, down_back)
    gelu_back = jax.vjp(partial(jax.nn.gelu, approximate=False), upper_in)[1]
    grad_upper = gelu_back(grad_hidden)[0].astype(jnp.bfloat16)
    grad_up = inner_rows(act_two, grad_upper)
    grad_up_bias = jnp.sum(grad_upper.astype(jnp.float32), axis=0)
    grad_act_two = times_trans(grad_upper, up_back)
    grad_in_two, grad_gain_two, grad_bias_two, grad_time_two = norm_backward(
        grad_act_two, normed_two, scales_two, inv_two, features
    )
    grad_middle = grad_final + grad_in_two
    mlp_gain, mlp_bias, mlp_time, mlp_up, mlp_up_bias, mlp_down, mlp_down_bias = (
        lax.psum_scatter(
            grad_gain_two.astype(jnp.bfloat16), "shard", scatter_dimension=0, tiled=True
        ).astype(jnp.float32),
        lax.psum_scatter(
            grad_bias_two.astype(jnp.bfloat16), "shard", scatter_dimension=0, tiled=True
        ).astype(jnp.float32),
        lax.psum_scatter(
            grad_time_two.astype(jnp.bfloat16), "shard", scatter_dimension=0, tiled=True
        ).astype(jnp.float32),
        lax.psum_scatter(
            grad_up.astype(jnp.bfloat16), "shard", scatter_dimension=0, tiled=True
        ).astype(jnp.float32),
        lax.psum_scatter(
            grad_up_bias.astype(jnp.bfloat16), "shard", scatter_dimension=0, tiled=True
        ).astype(jnp.float32),
        lax.psum_scatter(
            grad_down.astype(jnp.bfloat16), "shard", scatter_dimension=0, tiled=True
        ).astype(jnp.float32),
        lax.psum_scatter(
            grad_down_bias.astype(jnp.bfloat16), "shard", scatter_dimension=0, tiled=True
        ).astype(jnp.float32),
    )
    qkv_back, out_back = (
        lax.all_gather(qkv_weight, "shard", axis=0, tiled=True),
        lax.all_gather(out_weight, "shard", axis=0, tiled=True),
    )
    grad_branch = grad_middle.astype(jnp.bfloat16)
    grad_out_full = inner_rows(mixed_low, grad_branch)
    grad_mixed = times_trans(grad_branch, out_back).astype(jnp.bfloat16)
    grad_heads = grad_mixed.reshape(tok_rows, HEADS, HEAD)
    row_delta = jnp.transpose(jnp.sum(grad_heads.astype(jnp.float32) * mixed_sum, axis=2))
    zero_pair = jnp.zeros((2, tok_rows, width_d), jnp.float32)
    zero_query = jnp.zeros((tok_rows, HEADS, HEAD), jnp.float32)

    def return_step(running, block_item):
        kv_pair, key_seg, is_live = block_item

        def return_active(grad_query):
            prob_low, grad_scores = score_grads(
                query_heads, grad_heads, log_total, row_delta, kv_pair, own_seg, key_seg
            )
            key_heads = kv_pair[0].reshape(tok_rows, HEADS, HEAD)
            grad_query = grad_query + jnp.einsum(
                "hqk,khd->qhd", grad_scores, key_heads, preferred_element_type=jnp.float32
            )
            grad_key = jnp.einsum(
                "hqk,qhd->khd", grad_scores, query_heads, preferred_element_type=jnp.float32
            ).reshape(tok_rows, width_d)
            grad_value = jnp.einsum(
                "hqk,qhd->khd", prob_low, grad_heads, preferred_element_type=jnp.float32
            ).reshape(tok_rows, width_d)
            return (grad_query, jnp.stack([grad_key, grad_value]))

        def asleep(grad_query):
            return (grad_query, zero_pair)

        return lax.cond(is_live, return_active, asleep, running)

    grad_query, partials = lax.scan(return_step, zero_query, key_stacks)
    key_grads = partials[0]
    for order_num, shift_by in enumerate(offsets):
        key_grads = key_grads + send_back(partials[order_num + 1], shift_by)
    grad_joined = jnp.concatenate(
        [
            rotate(grad_query.reshape(tok_rows, width_d), -own_place),
            rotate(key_grads[0], -own_place),
            key_grads[1],
        ],
        axis=1,
    ).astype(jnp.bfloat16)
    grad_qkv_full = inner_rows(act_one, grad_joined)
    grad_act_one = times_trans(grad_joined, qkv_back)
    grad_in_one, grad_gain_one, grad_bias_one, grad_time_one = norm_backward(
        grad_act_one, normed_one, scales_one, inv_one, features
    )
    input_grad = grad_middle + grad_in_one
    attn_gain, attn_bias, attn_time, attn_qkv, attn_out = (
        lax.psum_scatter(
            grad_gain_one.astype(jnp.bfloat16), "shard", scatter_dimension=0, tiled=True
        ).astype(jnp.float32),
        lax.psum_scatter(
            grad_bias_one.astype(jnp.bfloat16), "shard", scatter_dimension=0, tiled=True
        ).astype(jnp.float32),
        lax.psum_scatter(
            grad_time_one.astype(jnp.bfloat16), "shard", scatter_dimension=0, tiled=True
        ).astype(jnp.float32),
        lax.psum_scatter(
            grad_qkv_full.astype(jnp.bfloat16), "shard", scatter_dimension=0, tiled=True
        ).astype(jnp.float32),
        lax.psum_scatter(
            grad_out_full.astype(jnp.bfloat16), "shard", scatter_dimension=0, tiled=True
        ).astype(jnp.float32),
    )
    summed = (
        lax.psum(attn_gain.astype(jnp.bfloat16), "ctx").astype(jnp.float32),
        lax.psum(attn_bias.astype(jnp.bfloat16), "ctx").astype(jnp.float32),
        lax.psum(attn_time.astype(jnp.bfloat16), "ctx").astype(jnp.float32),
        lax.psum(attn_qkv.astype(jnp.bfloat16), "ctx").astype(jnp.float32),
        lax.psum(attn_out.astype(jnp.bfloat16), "ctx").astype(jnp.float32),
        lax.psum(mlp_gain.astype(jnp.bfloat16), "ctx").astype(jnp.float32),
        lax.psum(mlp_bias.astype(jnp.bfloat16), "ctx").astype(jnp.float32),
        lax.psum(mlp_time.astype(jnp.bfloat16), "ctx").astype(jnp.float32),
        lax.psum(mlp_up.astype(jnp.bfloat16), "ctx").astype(jnp.float32),
        lax.psum(mlp_up_bias.astype(jnp.bfloat16), "ctx").astype(jnp.float32),
        lax.psum(mlp_down.astype(jnp.bfloat16), "ctx").astype(jnp.float32),
        lax.psum(mlp_down_bias.astype(jnp.bfloat16), "ctx").astype(jnp.float32),
    )
    return (
        block_out.astype(jnp.bfloat16)[None],
        loss_value,
        input_grad[None],
        summed[0],
        summed[1],
        summed[2],
        summed[3],
        summed[4],
        summed[5],
        summed[6],
        summed[7],
        summed[8],
        summed[9],
        summed[10],
        summed[11],
    )


def solution(mesh):
    in_specs = (
        P("shard", "ctx", None),
        P("shard", "ctx", None),
        P("shard", "ctx", None),
        P("shard", None),
        P("shard", None),
        P("shard", "ctx"),
        P("shard"),
        P("shard"),
        P("shard", None),
        P("shard", None),
        P("shard", None),
        P("shard"),
        P("shard"),
        P("shard", None),
        P("shard", None),
        P("shard"),
        P("shard", None),
        P("shard"),
    )
    out_specs = (
        P("shard", "ctx", None),
        P(),
        P("shard", "ctx", None),
        P("shard"),
        P("shard"),
        P("shard", None),
        P("shard", None),
        P("shard", None),
        P("shard"),
        P("shard"),
        P("shard", None),
        P("shard", None),
        P("shard"),
        P("shard", None),
        P("shard"),
    )
    return jax.shard_map(
        on_device, mesh=mesh, in_specs=in_specs, out_specs=out_specs, check_vma=False
    )
```

profile of v0, /device:TPU:0, one launch (start us, length us, event | category | flops | bytes accessed | tf_op | source)
XLA Modules:
  0.0 1912.5 jit_solution(11519160643120663605)
XLA Ops:
  19.6 11.8 all_gather.41
  36.3 58.0 %all-gather.10.cloned.1.call-done = bf16[1024,3072]{1,0:T(8,128)(2,1)} async-done(((bf16[512,3072]{1,0:T(8,128)(2,1)}), bf16[1024,3072]{1,0:T(8,128)(2,1)}) %all-gather.10.cloned.1.call-update) | async-done | bytes 6291472 | tf_op jit(solution)/shard_map/all_gather | solution.py:167
  180.0 12.7 all_gather.46
  194.3 40.6 %collective-permute-done.1 = bf16[2,512,1024]{2,1,0:T(8,128)(2,1)} collective-permute-done((bf16[2,512,1024]{2,1,0:T(8,128)(2,1)}, bf16[2,512,1024]{2,1,0:T(8,128)(2,1)}, u32[]{:S(2)}, u32[]{:S(2)}) %collective-permute-start.1) | collective-permute-done | bytes 2097184 | tf_op jit(solution)/shard_map/ppermute | solution.py:22
  236.3 40.9 %collective-permute-done.2 = bf16[2,512,1024]{2,1,0:T(8,128)(2,1)} collective-permute-done((bf16[2,512,1024]{2,1,0:T(8,128)(2,1)}, bf16[2,512,1024]{2,1,0:T(8,128)(2,1)}, u32[]{:S(2)}, u32[]{:S(2)}) %collective-permute-start.2) | collective-permute-done | bytes 2097184 | tf_op jit(solution)/shard_map/ppermute | solution.py:22
  304.0 65.0 %collective-permute-done.7 = bf16[2,512,1024]{2,1,0:T(8,128)(2,1)S(1)} collective-permute-done((bf16[2,512,1024]{2,1,0:T(8,128)(2,1)}, bf16[2,512,1024]{2,1,0:T(8,128)(2,1)S(1)}, u32[]{:S(2)}, u32[]{:S(2)}) %collective-permute-start.7) | collective-permute-done | bytes 2097184 | tf_op jit(solution)/shard_map/ppermute | solution.py:22
  370.5 25.4 %copy.77 = bf16[9,2,512,1024]{2,3,1,0:T(8,128)(2,1)} copy(bf16[9,2,512,1024]{3,2,1,0:T(8,128)(2,1)} %bitcast_dynamic-update-slice_fusion) | data formatting | bytes 37748736 | tf_op jit(solution)/shard_map/while | solution.py:219
  396.2 86.0 %while.29 = (s32[]{:T(128)}, f32[16,512]{1,0:T(8,128)S(1)}, f32[16,512]{1,0:T(8,128)S(1)}, f32[512,16,64]{0,2,1:T(8,128)S(1)}, pred[9]{0:T(512)(128)(4,1)S(1)}, ...) while((s32[]{:T(128)}, f32[16,512]{1,0:T(8,128)S(1)}, ...), condition=%wide.region_18.19_spmd, body=%wide.region_13.18_spmd.sunk | while | flops 1121214464 | bytes 130556192 | solution.py:219
  397.5 24.9 %conditional.4 = ((f32[16,512]{1,0:T(8,128)S(1)}, f32[16,512]{1,0:T(8,128)S(1)}, f32[512,16,64]{0,2,1:T(8,128)S(1)})) conditional(s32[]{:T(128)} %bitcast.253, (f32[16,512]{1,0:T(8,128)S(1)}, f32[16,512]{1,0:T(8,128)S(1)}, f32[512,16,64]{0,2,1:T(8,128)S(1)}) %tuple.140, (s32[512]{0:T(512)S(1)}, s32[9,512]{1,0:T(8,128)}, s32[]{:T(128)}, ...), branch_computations={%region_14.14_spmd, %region_15.17_spmd} | conditional | flops 1121214464 | bytes 130555992 | solution.py:214
  413.1 9.2 fusion.1
  428.7 24.9 %conditional.4 = ((f32[16,512]{1,0:T(8,128)S(1)}, f32[16,512]{1,0:T(8,128)S(1)}, f32[512,16,64]{0,2,1:T(8,128)S(1)})) conditional(s32[]{:T(128)} %bitcast.253, (f32[16,512]{1,0:T(8,128)S(1)}, f32[16,512]{1,0:T(8,128)S(1)}, f32[512,16,64]{0,2,1:T(8,128)S(1)}) %tuple.140, (s32[512]{0:T(512)S(1)}, s32[9,512]{1,0:T(8,128)}, s32[]{:T(128)}, ...), branch_computations={%region_14.14_spmd, %region_15.17_spmd} | conditional | flops 1121214464 | bytes 130555992 | solution.py:214
  444.4 9.2 fusion.1
  454.9 24.9 %conditional.4 = ((f32[16,512]{1,0:T(8,128)S(1)}, f32[16,512]{1,0:T(8,128)S(1)}, f32[512,16,64]{0,2,1:T(8,128)S(1)})) conditional(s32[]{:T(128)} %bitcast.253, (f32[16,512]{1,0:T(8,128)S(1)}, f32[16,512]{1,0:T(8,128)S(1)}, f32[512,16,64]{0,2,1:T(8,128)S(1)}) %tuple.140, (s32[512]{0:T(512)S(1)}, s32[9,512]{1,0:T(8,128)}, s32[]{:T(128)}, ...), branch_computations={%region_14.14_spmd, %region_15.17_spmd} | conditional | flops 1121214464 | bytes 130555992 | solution.py:214
  470.5 9.2 fusion.1
  490.2 26.5 %multiply_convert_fusion = (bf16[512,4096]{1,0:T(8,128)(2,1)}, f32[512,4096]{1,0:T(8,128)}, f32[512,4096]{1,0:T(8,128)}) fusion(f32[4096]{0:T(1024)S(1)} %copy-done.49, bf16[512,1024]{1,0:T(8,128)(2,1)} %get-tuple-element.514, bf16[1024,4096]{1,0:T(8,128)(2,1)} %all-gather.14.cloned.1.call-done), kind=kOutput, calls=%fused_computation.38 | convolution fusion | flops 4433379328 | bytes 30425088 | tf_op jit(solution)/shard_map/dot_general | solution.py:240
  516.7 11.3 fusion.50
  528.0 134.4 %all-reduce.6 = (f32[]{:T(128)}, f32[]{:T(128)}) all-reduce(f32[]{:T(128)} %get-tuple-element.517, f32[]{:T(128)} %convert_reduce_fusion.9), channel_id=1, replica_groups=mesh['ctx'=16,'shard'=2] {'ctx','shard'}, use_global_device_ids=true, to_apply=%region_22.23 | all-reduce | flops 2 | bytes 16 | tf_op jit(solution)/shard_map/psum | solution.py:251
  666.4 15.7 fusion.79
  682.1 11.8 fusion.74
  705.8 201.3 %while.30 = (s32[]{:T(128)}, f32[512,16,64]{0,2,1:T(8,128)}, f32[9,2,512,1024]{2,3,1,0:T(8,128)}, pred[9]{0:T(512)(128)(4,1)S(1)}, s32[512]{0:T(512)S(1)}, /*ind...) while((s32[]{:T(128)}, f32[512,16,64]{0,2,1:T(8,128)}, ...), condition=%wide.region_31.32_spmd, body=%wide.region_28.31_spmd.sunk | while | flops 2732326912 | bytes 184525664 | solution.py:335
  707.4 44.3 %conditional.5 = (f32[512,16,64]{0,2,1:T(8,128)}, f32[1,2,512,1024]{2,3,1,0:T(8,128)}) conditional(s32[]{:T(128)} %bitcast.254, f32[512,16,64]{0,2,1:T(8,128)} %get-tuple-element.715, (s32[512]{0:T(512)S(1)}, s32[9,512]{1,0:T(8,128)}, s32[]{:T(128)}, bf16[9,2,512,1024]{2,3,1,0:T(8,128)(2,1)}, bf16[512,16,64]{0,2,1:T(8,128)(2,1)S(1)}, ...), branch_computations={%region_29.29_spmd, %region_30.30_spmd} | conditional | flops 2732326912 | bytes 176136336 | solution.py:333
  709.1 8.2 fusion.92
  718.3 9.4 fusion.12
  732.0 9.2 fusion.16
  791.1 44.3 %conditional.5 = (f32[512,16,64]{0,2,1:T(8,128)}, f32[1,2,512,1024]{2,3,1,0:T(8,128)}) conditional(s32[]{:T(128)} %bitcast.254, f32[512,16,64]{0,2,1:T(8,128)} %get-tuple-element.715, (s32[512]{0:T(512)S(1)}, s32[9,512]{1,0:T(8,128)}, s32[]{:T(128)}, bf16[9,2,512,1024]{2,3,1,0:T(8,128)(2,1)}, bf16[512,16,64]{0,2,1:T(8,128)(2,1)S(1)}, ...), branch_computations={%region_29.29_spmd, %region_30.30_spmd} | conditional | flops 2732326912 | bytes 176136336 | solution.py:333
  792.9 8.2 fusion.92
  802.0 9.4 fusion.12
  815.7 9.2 fusion.16
  841.3 44.2 %conditional.5 = (f32[512,16,64]{0,2,1:T(8,128)}, f32[1,2,512,1024]{2,3,1,0:T(8,128)}) conditional(s32[]{:T(128)} %bitcast.254, f32[512,16,64]{0,2,1:T(8,128)} %get-tuple-element.715, (s32[512]{0:T(512)S(1)}, s32[9,512]{1,0:T(8,128)}, s32[]{:T(128)}, bf16[9,2,512,1024]{2,3,1,0:T(8,128)(2,1)}, bf16[512,16,64]{0,2,1:T(8,128)(2,1)S(1)}, ...), branch_computations={%region_29.29_spmd, %region_30.30_spmd} | conditional | flops 2732326912 | bytes 176136336 | solution.py:333
  843.0 8.2 fusion.92
  852.2 9.4 fusion.12
  865.8 9.2 fusion.16
  907.1 13.4 convert.67
  931.8 171.8 %collective-permute-start.13 = (bf16[2,512,1024]{1,2,0:T(8,128)(2,1)}, bf16[2,512,1024]{1,2,0:T(8,128)(2,1)}, u32[]{:S(2)}, u32[]{:S(2)}) collective-permute-start(bf16[2,512,1024]{1,2,0:T(8,128)(2,1)} %get-tuple-element.458), channel_id=1, source_target_pairs={{0,4},{2,6},{4,8},{6,10},{8,12},{10,14},{12,16},{14,18},{16,20},{1... | collective-permute-start | bytes 6291464 | tf_op jit(solution)/shard_map/ppermute | solution.py:22
  1120.3 68.9 %collective-permute-done.13 = bf16[2,512,1024]{1,2,0:T(8,128)(2,1)} collective-permute-done((bf16[2,512,1024]{1,2,0:T(8,128)(2,1)}, bf16[2,512,1024]{1,2,0:T(8,128)(2,1)}, u32[]{:S(2)}, u32[]{:S(2)}) %collective-permute-start.13) | collective-permute-done | bytes 2097184 | tf_op jit(solution)/shard_map/ppermute | solution.py:22
  1189.2 89.8 %collective-permute-done.14 = bf16[2,512,1024]{1,2,0:T(8,128)(2,1)} collective-permute-done((bf16[2,512,1024]{1,2,0:T(8,128)(2,1)}, bf16[2,512,1024]{1,2,0:T(8,128)(2,1)}, u32[]{:S(2)}, u32[]{:S(2)}) %collective-permute-start.14) | collective-permute-done | bytes 2097184 | tf_op jit(solution)/shard_map/ppermute | solution.py:22
  1279.0 8.3 fusion.33
  1290.9 8.8 fusion.75
  1305.4 8.5 convolution_convert_fusion.2
  1314.0 10.5 convolution_convert_fusion
  1324.8 10.7 convolution_convert_fusion.1
  1335.6 15.0 reduce-scatter.11.cloned.1.call-done
  1350.6 80.1 %reduce-scatter.9.cloned.1.call-done = bf16[512,3072]{1,0:T(8,128)(2,1)} async-done(((bf16[1024,3072]{1,0:T(8,128)(2,1)}), bf16[512,3072]{1,0:T(8,128)(2,1)}) %reduce-scatter.9.cloned.1.call-update) | async-done | bytes 3145744 | tf_op jit(solution)/shard_map/reduce_scatter | solution.py:363
  1430.7 102.2 %reduce-scatter.17.cloned.1.call-done = bf16[2048,1024]{1,0:T(8,128)(2,1)} async-done(((bf16[4096,1024]{1,0:T(8,128)(2,1)}), bf16[2048,1024]{1,0:T(8,128)(2,1)}) %reduce-scatter.17.cloned.1.call-update) | async-done | bytes 4194320 | tf_op jit(solution)/shard_map/reduce_scatter | solution.py:292
  1532.8 102.1 %reduce-scatter.15.cloned.1.call-done = bf16[512,4096]{1,0:T(8,128)(2,1)} async-done(((bf16[1024,4096]{1,0:T(8,128)(2,1)}), bf16[512,4096]{1,0:T(8,128)(2,1)}) %reduce-scatter.15.cloned.1.call-update) | async-done | bytes 4194320 | tf_op jit(solution)/shard_map/reduce_scatter | solution.py:286
  1638.1 7.1 all-reduce.9
  1645.5 35.5 %all-reduce.7 = (bf16[512]{0:T(512)(128)(2,1)S(1)}, bf16[512]{0:T(512)(128)(2,1)S(1)}, bf16[512]{0:T(512)(128)(2,1)S(1)}, bf16[512]{0:T(512)(128)(2,1)S(1)}, bf1...) all-reduce(bf16[512]{0:T(512)(128)(2,1)S(1)} %dynamic-slice.1, ...), channel_id=1, replica_groups=mesh['ctx'=16,'shard'=2] {'ctx'}, use_global_device_ids=true, to_apply=%region_36.37 | all-reduce | flops 4608 | bytes 18432 | tf_op jit(solution)/shard_map/psum | solution.py:371
  1688.1 198.5 %all-reduce.12.cloned.1.call-done = (bf16[128,1024]{1,0:T(8,128)(2,1)}, bf16[512,3072]{1,0:T(8,128)(2,1)}, bf16[512,1024]{1,0:T(8,128)(2,1)}, bf16[128,1024]{1,0...) async-done(((bf16[128,1024]{1,0:T(8,128)(2,1)}, bf16[512,3072]{1,0:T(8,128)(2,1)}, bf16[512,1024]{1,0:T(8,128)(2,1)}, bf16[128,1024]{1,0:T(8,128)(2,1)}, ...) | async-done | bytes 13107216 | tf_op jit(solution)/shard_map/psum | solution.py:373
  (422 shorter events, 382.4 us)
Async XLA Ops:
  7.2 24.2 %copy-start.5 = (bf16[1,512,1024]{2,1,0:T(8,128)(2,1)S(1)}, bf16[1,512,1024]{2,1,0:T(8,128)(2,1)}, u32[]{:S(2)}) copy-start(bf16[1,512,1024]{2,1,0:T(8,128)(2,1)} %param.26) | copy-start | bytes 3145732
  7.2 87.1 %all-gather.10.cloned.1.call-start = ((), (), s32[]{:S(2)}) async-start(), calls=%async_computation.6 | async-start | bytes 9437184 | tf_op jit(solution)/shard_map/all_gather | solution.py:167
  8.0 475.8 %all-gather.12.cloned.1.call-start = ((), (), s32[]{:S(2)}) async-start(), calls=%async_computation.7 | async-start | bytes 3145728 | tf_op jit(solution)/shard_map/all_gather | solution.py:168
  8.7 481.4 %all-gather.14.cloned.1.call-start = ((), (), s32[]{:S(2)}) async-start(), calls=%async_computation.8 | async-start | bytes 12582912 | tf_op jit(solution)/shard_map/all_gather | solution.py:230
  9.5 507.2 %all-gather.16.cloned.1.call-start = ((), (), s32[]{:S(2)}) async-start(), calls=%async_computation.9 | async-start | bytes 12582912 | tf_op jit(solution)/shard_map/all_gather | solution.py:232
  15.2 21.1 %copy-start.50 = (f32[2,1,512]{2,1,0:T(1,128)}, f32[2,1,512]{2,1,0:T(1,128)S(1)}, u32[]{:S(2)}) copy-start(f32[2,1,512]{2,1,0:T(1,128)S(1)} %convert_element_type.413) | copy-start | bytes 12292
  31.6 68.2 %copy-start.40 = (f32[512]{0:T(512)}, f32[512]{0:T(512)S(1)}, u32[]{:S(2)}) copy-start(f32[512]{0:T(512)S(1)} %broadcast_multiply_fusion.6) | copy-start | bytes 6148
  32.1 67.8 %copy-start.44 = (f32[512]{0:T(512)}, f32[512]{0:T(512)S(1)}, u32[]{:S(2)}) copy-start(f32[512]{0:T(512)S(1)} %add_rsqrt_fusion.1) | copy-start | bytes 6148
  36.3 63.5 %copy-start.32 = (bf16[512,1024]{1,0:T(8,128)(2,1)}, bf16[512,1024]{1,0:T(8,128)(2,1)S(1)}, u32[]{:S(2)}) copy-start(bf16[512,1024]{1,0:T(8,128)(2,1)S(1)} %get-tuple-element.510) | copy-start | bytes 3145732
  113.6 22.7 %copy-start.53 = (s32[1,512]{1,0:T(1,128)S(1)}, s32[1,512]{1,0:T(1,128)}, u32[]{:S(2)}) copy-start(s32[1,512]{1,0:T(1,128)} %param.31) | copy-start | bytes 6148
  113.6 46.3 %copy-start.62 = (bf16[512]{0:T(512)(128)(2,1)S(1)}, bf16[512]{0:T(512)(128)(2,1)}, u32[]{:S(2)}) copy-start(bf16[512]{0:T(512)(128)(2,1)} %param.37) | copy-start | bytes 3076
  113.6 50.7 %copy-start.63 = (bf16[512]{0:T(512)(128)(2,1)S(1)}, bf16[512]{0:T(512)(128)(2,1)}, u32[]{:S(2)}) copy-start(bf16[512]{0:T(512)(128)(2,1)} %param.38) | copy-start | bytes 3076
  113.6 55.1 %copy-start.56 = (bf16[2048]{0:T(1024)(128)(2,1)S(1)}, bf16[2048]{0:T(1024)(128)(2,1)}, u32[]{:S(2)}) copy-start(bf16[2048]{0:T(1024)(128)(2,1)} %param.41) | copy-start | bytes 12292
  113.6 60.1 %copy-start.64 = (bf16[512]{0:T(512)(128)(2,1)S(1)}, bf16[512]{0:T(512)(128)(2,1)}, u32[]{:S(2)}) copy-start(bf16[512]{0:T(512)(128)(2,1)} %param.43) | copy-start | bytes 3076
  113.7 66.4 %copy-start.37 = (bf16[128,1024]{1,0:T(8,128)(2,1)S(1)}, bf16[128,1024]{1,0:T(8,128)(2,1)}, u32[]{:S(2)}) copy-start(bf16[128,1024]{1,0:T(8,128)(2,1)} %param.39) | copy-start | bytes 786436
  115.2 21.8 %collective-permute-start = (bf16[2,512,1024]{2,1,0:T(8,128)(2,1)}, bf16[2,512,1024]{2,1,0:T(8,128)(2,1)}, u32[]{:S(2)}, u32[]{:S(2)}) collective-permute-start(bf16[2,512,1024]{2,1,0:T(8,128)(2,1)} %pad_maximum_fusion.1), channel_id=1, source_target_pairs={{0,2},{2,4},{4,6},{6,8},{8,10},{10,12},{12,14},{14,16},{16,18},{18... | collective-permute-start | bytes 6291464 | tf_op jit(solution)/shard_map/ppermute | solution.py:22
  118.6 1217.0 %reduce-scatter.13.cloned.1.call-start = ((), (), s32[]{:S(2)}) async-start(), calls=%async_computation.13 | async-start | bytes 786432 | tf_op jit(solution)/shard_map/reduce_scatter | solution.py:283
  118.6 116.3 %collective-permute-start.1 = (bf16[2,512,1024]{2,1,0:T(8,128)(2,1)}, bf16[2,512,1024]{2,1,0:T(8,128)(2,1)}, u32[]{:S(2)}, u32[]{:S(2)}) collective-permute-start(bf16[2,512,1024]{2,1,0:T(8,128)(2,1)} %pad_maximum_fusion.1), channel_id=1, source_target_pairs={{0,4},{2,6},{4,8},{6,10},{8,12},{10,14},{12,16},{14,18},{16,20},{1... | collective-permute-start | bytes 6291464 | tf_op jit(solution)/shard_map/ppermute | solution.py:22
  123.0 154.2 %collective-permute-start.2 = (bf16[2,512,1024]{2,1,0:T(8,128)(2,1)}, bf16[2,512,1024]{2,1,0:T(8,128)(2,1)}, u32[]{:S(2)}, u32[]{:S(2)}) collective-permute-start(bf16[2,512,1024]{2,1,0:T(8,128)(2,1)} %pad_maximum_fusion.1), channel_id=1, source_target_pairs={{0,6},{2,8},{4,10},{6,12},{8,14},{10,16},{12,18},{14,20},{16,22},{... | collective-permute-start | bytes 6291464 | tf_op jit(solution)/shard_map/ppermute | solution.py:22
  130.3 157.5 %collective-permute-start.3 = (bf16[2,512,1024]{2,1,0:T(8,128)(2,1)}, bf16[2,512,1024]{2,1,0:T(8,128)(2,1)}, u32[]{:S(2)}, u32[]{:S(2)}) collective-permute-start(bf16[2,512,1024]{2,1,0:T(8,128)(2,1)} %pad_maximum_fusion.1), channel_id=1, source_target_pairs={{0,8},{2,10},{4,12},{6,14},{8,16},{10,18},{12,20},{14,22},{16,24},... | collective-permute-start | bytes 6291464 | tf_op jit(solution)/shard_map/ppermute | solution.py:22
  134.4 156.5 %collective-permute-start.4 = (bf16[2,512,1024]{2,1,0:T(8,128)(2,1)}, bf16[2,512,1024]{2,1,0:T(8,128)(2,1)}, u32[]{:S(2)}, u32[]{:S(2)}) collective-permute-start(bf16[2,512,1024]{2,1,0:T(8,128)(2,1)} %pad_maximum_fusion.1), channel_id=1, source_target_pairs={{2,0},{4,2},{6,4},{8,6},{10,8},{12,10},{14,12},{16,14},{18,16},{20... | collective-permute-start | bytes 6291464 | tf_op jit(solution)/shard_map/ppermute | solution.py:22
  137.0 157.1 %collective-permute-start.5 = (bf16[2,512,1024]{2,1,0:T(8,128)(2,1)}, bf16[2,512,1024]{2,1,0:T(8,128)(2,1)}, u32[]{:S(2)}, u32[]{:S(2)}) collective-permute-start(bf16[2,512,1024]{2,1,0:T(8,128)(2,1)} %pad_maximum_fusion.1), channel_id=1, source_target_pairs={{4,0},{6,2},{8,4},{10,6},{12,8},{14,10},{16,12},{18,14},{20,16},{2... | collective-permute-start | bytes 6291464 | tf_op jit(solution)/shard_map/ppermute | solution.py:22
  234.9 67.6 %collective-permute-start.6 = (bf16[2,512,1024]{2,1,0:T(8,128)(2,1)}, bf16[2,512,1024]{2,1,0:T(8,128)(2,1)S(1)}, u32[]{:S(2)}, u32[]{:S(2)}) collective-permute-start(bf16[2,512,1024]{2,1,0:T(8,128)(2,1)} %pad_maximum_fusion.1), channel_id=1, source_target_pairs={{6,0},{8,2},{10,4},{12,6},{14,8},{16,10},{18,12},{20,14},{22,16},{... | collective-permute-start | bytes 6291464 | tf_op jit(solution)/shard_map/ppermute | solution.py:22
  277.2 91.8 %collective-permute-start.7 = (bf16[2,512,1024]{2,1,0:T(8,128)(2,1)}, bf16[2,512,1024]{2,1,0:T(8,128)(2,1)S(1)}, u32[]{:S(2)}, u32[]{:S(2)}) collective-permute-start(bf16[2,512,1024]{2,1,0:T(8,128)(2,1)} %pad_maximum_fusion.1), channel_id=1, source_target_pairs={{8,0},{10,2},{12,4},{14,6},{16,8},{18,10},{20,12},{22,14},{24,16},... | collective-permute-start | bytes 6291464 | tf_op jit(solution)/shard_map/ppermute | solution.py:22
  487.6 206.4 %copy-start.3 = (f32[512,1024]{1,0:T(8,128)}, f32[512,1024]{1,0:T(8,128)S(1)}, u32[]{:S(2)}) copy-start(f32[512,1024]{1,0:T(8,128)S(1)} %get-tuple-element.513) | copy-start | bytes 6291460
  487.6 206.3 %copy-start.42 = (f32[512]{0:T(512)}, f32[512]{0:T(512)S(1)}, u32[]{:S(2)}) copy-start(f32[512]{0:T(512)S(1)} %broadcast_multiply_fusion.5) | copy-start | bytes 6148
  488.0 206.0 %copy-start.47 = (f32[512]{0:T(512)}, f32[512]{0:T(512)S(1)}, u32[]{:S(2)}) copy-start(f32[512]{0:T(512)S(1)} %add_rsqrt_fusion) | copy-start | bytes 6148
  490.2 26.5 %copy-start.55 = (f32[1,512]{1,0:T(1,128)S(1)}, f32[1,512]{1,0:T(1,128)}, u32[]{:S(2)}) copy-start(f32[1,512]{1,0:T(1,128)} %convert_element_type.357) | copy-start | bytes 6148
  490.2 26.5 %copy-start.57 = (f32[2,1,512]{2,1,0:T(1,128)S(1)}, f32[2,1,512]{2,1,0:T(1,128)}, u32[]{:S(2)}) copy-start(f32[2,1,512]{2,1,0:T(1,128)} %convert_element_type.417) | copy-start | bytes 12292
  666.4 15.7 copy-start.33
  666.4 15.7 copy-start.24
  920.4 196.6 %copy-start.4 = (f32[512,1024]{1,0:T(8,128)S(1)}, f32[512,1024]{1,0:T(8,128)}, u32[]{:S(2)}) copy-start(f32[512,1024]{1,0:T(8,128)} %copy-done.3) | copy-start | bytes 6291460
  920.4 196.6 %copy-start.43 = (f32[512]{0:T(512)S(1)}, f32[512]{0:T(512)}, u32[]{:S(2)}) copy-start(f32[512]{0:T(512)} %copy-done.42) | copy-start | bytes 6148
  920.4 196.6 %copy-start.48 = (f32[512]{0:T(512)S(1)}, f32[512]{0:T(512)}, u32[]{:S(2)}) copy-start(f32[512]{0:T(512)} %copy-done.47) | copy-start | bytes 6148
  926.4 184.1 %collective-permute-start.10 = (bf16[2,512,1024]{1,2,0:T(8,128)(2,1)}, bf16[2,512,1024]{1,2,0:T(8,128)(2,1)}, u32[]{:S(2)}, u32[]{:S(2)}) collective-permute-start(bf16[2,512,1024]{1,2,0:T(8,128)(2,1)} %get-tuple-element.461), channel_id=1, source_target_pairs={{6,0},{8,2},{10,4},{12,6},{14,8},{16,10},{18,12},{20,14},{22,16},{... | collective-permute-start | bytes 6291464 | tf_op jit(solution)/shard_map/ppermute | solution.py:22
  927.7 186.7 %collective-permute-start.11 = (bf16[2,512,1024]{1,2,0:T(8,128)(2,1)}, bf16[2,512,1024]{1,2,0:T(8,128)(2,1)}, u32[]{:S(2)}, u32[]{:S(2)}) collective-permute-start(bf16[2,512,1024]{1,2,0:T(8,128)(2,1)} %get-tuple-element.460), channel_id=1, source_target_pairs={{8,0},{10,2},{12,4},{14,6},{16,8},{18,10},{20,12},{22,14},{24,16},... | collective-permute-start | bytes 6291464 | tf_op jit(solution)/shard_map/ppermute | solution.py:22
  929.0 186.7 %collective-permute-start.12 = (bf16[2,512,1024]{1,2,0:T(8,128)(2,1)}, bf16[2,512,1024]{1,2,0:T(8,128)(2,1)}, u32[]{:S(2)}, u32[]{:S(2)}) collective-permute-start(bf16[2,512,1024]{1,2,0:T(8,128)(2,1)} %get-tuple-element.459), channel_id=1, source_target_pairs={{0,2},{2,4},{4,6},{6,8},{8,10},{10,12},{12,14},{14,16},{16,18},{18... | collective-permute-start | bytes 6291464 | tf_op jit(solution)/shard_map/ppermute | solution.py:22
  931.8 257.4 %collective-permute-start.13 = (bf16[2,512,1024]{1,2,0:T(8,128)(2,1)}, bf16[2,512,1024]{1,2,0:T(8,128)(2,1)}, u32[]{:S(2)}, u32[]{:S(2)}) collective-permute-start(bf16[2,512,1024]{1,2,0:T(8,128)(2,1)} %get-tuple-element.458), channel_id=1, source_target_pairs={{0,4},{2,6},{4,8},{6,10},{8,12},{10,14},{12,16},{14,18},{16,20},{1... | collective-permute-start | bytes 6291464 | tf_op jit(solution)/shard_map/ppermute | solution.py:22
  1103.7 175.3 %collective-permute-start.14 = (bf16[2,512,1024]{1,2,0:T(8,128)(2,1)}, bf16[2,512,1024]{1,2,0:T(8,128)(2,1)}, u32[]{:S(2)}, u32[]{:S(2)}) collective-permute-start(bf16[2,512,1024]{1,2,0:T(8,128)(2,1)} %get-tuple-element.457), channel_id=1, source_target_pairs={{0,6},{2,8},{4,10},{6,12},{8,14},{10,16},{12,18},{14,20},{16,22},{... | collective-permute-start | bytes 6291464 | tf_op jit(solution)/shard_map/ppermute | solution.py:22
  1110.5 168.5 %collective-permute-start.15 = (bf16[2,512,1024]{1,2,0:T(8,128)(2,1)}, bf16[2,512,1024]{1,2,0:T(8,128)(2,1)}, u32[]{:S(2)}, u32[]{:S(2)}) collective-permute-start(bf16[2,512,1024]{1,2,0:T(8,128)(2,1)} %get-tuple-element.456), channel_id=1, source_target_pairs={{0,8},{2,10},{4,12},{6,14},{8,16},{10,18},{12,20},{14,22},{16,24},... | collective-permute-start | bytes 6291464 | tf_op jit(solution)/shard_map/ppermute | solution.py:22
  1114.4 164.6 %collective-permute-start.8 = (bf16[2,512,1024]{1,2,0:T(8,128)(2,1)}, bf16[2,512,1024]{1,2,0:T(8,128)(2,1)}, u32[]{:S(2)}, u32[]{:S(2)}) collective-permute-start(bf16[2,512,1024]{1,2,0:T(8,128)(2,1)} %get-tuple-element.455), channel_id=1, source_target_pairs={{2,0},{4,2},{6,4},{8,6},{10,8},{12,10},{14,12},{16,14},{18,16},{20... | collective-permute-start | bytes 6291464 | tf_op jit(solution)/shard_map/ppermute | solution.py:22
  1115.7 163.3 %collective-permute-start.9 = (bf16[2,512,1024]{1,2,0:T(8,128)(2,1)}, bf16[2,512,1024]{1,2,0:T(8,128)(2,1)}, u32[]{:S(2)}, u32[]{:S(2)}) collective-permute-start(bf16[2,512,1024]{1,2,0:T(8,128)(2,1)} %get-tuple-element.462), channel_id=1, source_target_pairs={{4,0},{6,2},{8,4},{10,6},{12,8},{14,10},{16,12},{18,14},{20,16},{2... | collective-permute-start | bytes 6291464 | tf_op jit(solution)/shard_map/ppermute | solution.py:22
  1120.3 215.3 %reduce-scatter.7.cloned.1.call-start = ((), (), s32[]{:S(2)}) async-start(), calls=%async_computation.10 | async-start | bytes 786432 | tf_op jit(solution)/shard_map/reduce_scatter | solution.py:360
  1301.2 49.4 %reduce-scatter.11.cloned.1.call-start = ((), (), s32[]{:S(2)}) async-start(), calls=%async_computation.12 | async-start | bytes 3145728 | tf_op jit(solution)/shard_map/reduce_scatter | solution.py:366
  1305.1 125.5 %reduce-scatter.9.cloned.1.call-start = ((), (), s32[]{:S(2)}) async-start(), calls=%async_computation.11 | async-start | bytes 9437184 | tf_op jit(solution)/shard_map/reduce_scatter | solution.py:363
  1313.9 218.9 %reduce-scatter.17.cloned.1.call-start = ((), (), s32[]{:S(2)}) async-start(), calls=%async_computation.15 | async-start | bytes 12582912 | tf_op jit(solution)/shard_map/reduce_scatter | solution.py:292
  1324.5 310.4 %reduce-scatter.15.cloned.1.call-start = ((), (), s32[]{:S(2)}) async-start(), calls=%async_computation.14 | async-start | bytes 12582912 | tf_op jit(solution)/shard_map/reduce_scatter | solution.py:286
  1335.5 551.1 %all-reduce.12.cloned.1.call-start = ((), (), s32[]{:S(2)}) async-start(), calls=%async_computation.16 | async-start | bytes 26214400 | tf_op jit(solution)/shard_map/psum | solution.py:373
  (57 other events, 293.4 us)
Sparse Core Ops, SparseCore 0:
  9.6 84.6 all-gather.9
  95.9 34.3 all-gather.11
  131.8 109.8 all-gather.13
  243.1 103.9 all-gather.15
  1120.4 92.5 reduce-scatter.12
  1301.3 14.5 reduce-scatter.6
  1318.7 31.8 reduce-scatter.10
  1353.6 77.0 reduce-scatter.8
  1433.6 99.2 reduce-scatter.16
  1535.7 99.2 reduce-scatter.14
  1640.2 246.3 all-reduce.11
where the time goes:
time: 1910 us
  waiting for transfers between devices  869 us (45%)
  matrix products  255 us (13%)
  blocking collectives  229 us (12%)
  starting transfers between devices  212 us (11%)
  local copies, waits for them, and re-layouts  183 us (10%)
  other arithmetic  114 us (6%)
  between operations  39.4 us (2%)
    ppermute x16, waiting for transfers between devices, from_behind(): return lax.ppermute(x, axis, pairs)  311 us
    ppermute x16, starting transfers between devices, from_behind(): return lax.ppermute(x, axis, pairs)  211 us
    psum x1, waiting for transfers between devices, on_device(): lax.psum(attn_time.astype(jnp.bfloat16), 'ctx').astype(jnp.float32)  198 us
    psum x1, blocking collectives, on_device(): lax.psum((jnp.sum(weight_mask[:, None] * misfit * misfit), jnp.sum(weight...  134 us
    reduce_scatter x1, waiting for transfers between devices, on_device(): lax.psum_scatter(grad_down.astype(jnp.bfloat16), 'shard', scatter_dimensi...  102 us
    reduce_scatter x1, waiting for transfers between devices, on_device(): lax.psum_scatter(grad_up.astype(jnp.bfloat16), 'shard', scatter_dimension...  102 us
    reduce_scatter x1, waiting for transfers between devices, on_device(): lax.psum_scatter(grad_qkv_full.astype(jnp.bfloat16), 'shard', scatter_dim...  80.1 us
    all_gather x1, waiting for transfers between devices, on_device(): lax.all_gather(qkv_weight, 'shard', axis=0, tiled=True)  58 us
  transfers between devices with their start and end apart: 27, of which 12 were waited for; matrix products, arithmetic and copies ran while one was open for 13% of the time, Pallas kernels for 0%

commit v1 on v0

v1 whole, which is shorter than its diff:
```python
import math

import jax
import jax.numpy as jnp
from jax import lax
from jax.experimental import pallas as pl
from jax.experimental.pallas import tpu as pltpu
from jax.sharding import Mesh
from jax.sharding import PartitionSpec as P

HEADS = 16
HEAD = 64
TEMB = 256
QUAD = 4
LOCAL_HEADS = HEADS // QUAD
LANES = 128
BLOCK_Q = 256
BLOCK_K = 256
norm_eps = 1e-05
masked_value = -1e30
LOG2E = math.log2(math.e)
bf16 = jnp.bfloat16
f32 = jnp.float32


def flip(value, axis):
    return lax.ppermute(value, axis, [(0, 1), (1, 0)])


def in_order(index, own, other, axis):
    return jnp.where(
        index == 0,
        jnp.concatenate([own, other], axis=axis),
        jnp.concatenate([other, own], axis=axis),
    )


def half_of(value, index):
    rows = value.shape[0] // 2
    return lax.dynamic_slice_in_dim(value, index * rows, rows, 0)


def xor_pairs(size, bit):
    return [(i, i ^ bit) for i in range(size)]


def bits_of(axis):
    return [1 << b for b in range(lax.axis_size(axis).bit_length() - 1)]


def scatter_sum(value, axis):
    size = lax.axis_size(axis)
    for bit in bits_of(axis):
        mine = (lax.axis_index(axis) // bit) % 2
        sent = half_of(value, 1 - mine).astype(bf16)
        got = lax.ppermute(sent, axis, xor_pairs(size, bit))
        value = half_of(value, mine).astype(f32) + got.astype(f32)
    return value


def gather_back(value, axis):
    size = lax.axis_size(axis)
    for bit in reversed(bits_of(axis)):
        mine = (lax.axis_index(axis) // bit) % 2
        got = lax.ppermute(value, axis, xor_pairs(size, bit))
        value = in_order(mine, value, got, 0)
    return value


def sum_all(value, axis):
    size = lax.axis_size(axis)
    for bit in bits_of(axis):
        value = value + lax.ppermute(value, axis, xor_pairs(size, bit))
    return value


def gather_shard(value):
    if lax.axis_size("shard") == 2:
        return in_order(lax.axis_index("shard"), value, flip(value, "shard"), 0)
    return lax.all_gather(value, "shard", axis=0, tiled=True)


def contract_rows(left_side, right_side):
    return lax.dot_general(
        left_side, right_side, (((0,), (0,)), ((), ())), preferred_element_type=f32
    )


def times_trans(left_side, right_side):
    return lax.dot_general(
        left_side, right_side, (((1,), (1,)), ((), ())), preferred_element_type=f32
    )


def times(left_side, right_side):
    return jnp.dot(left_side, right_side, preferred_element_type=f32)


def segments_at(starts, places):
    return jnp.sum((starts[None, :] <= places[:, None]).astype(jnp.int32), axis=1) - 1


def begins_at(starts, places):
    return jnp.max(jnp.where(starts[None, :] <= places[:, None], starts[None, :], 0), axis=1)


def ends_at(starts, places, length):
    return jnp.min(jnp.where(starts[None, :] > places[:, None], starts[None, :], length), axis=1)


def block_ranges(starts, length, row_base, row_block, col_base, col_block, tokens):
    count = tokens // row_block
    first = row_base + row_block * jnp.arange(count, dtype=jnp.int32)
    last = first + row_block - 1
    real = jnp.logical_and(first >= 0, last < length)
    begin_first = begins_at(starts, first)
    low = jnp.clip(begin_first - col_base, 0, tokens)
    high = jnp.clip(ends_at(starts, last, length) - col_base, 0, tokens)
    live = jnp.logical_and(real, high > low)
    low_block = jnp.where(live, low // col_block, 0)
    high_block = jnp.where(live, (high + col_block - 1) // col_block, 0)
    whole = jnp.logical_and(live, begin_first == begins_at(starts, last))
    full_low = jnp.where(whole, (low + col_block - 1) // col_block, high_block)
    full_high = jnp.where(whole, high // col_block, high_block)
    full_low = jnp.minimum(full_low, high_block)
    full_high = jnp.clip(full_high, full_low, high_block)
    return jnp.stack([low_block, full_low, full_high, high_block]).astype(jnp.int32)


def time_features(time_index):
    halfway = TEMB // 2
    ladder = jnp.exp(-math.log(10000.0) * jnp.arange(halfway, dtype=f32) / halfway)
    phases = time_index.astype(f32)[:, None] * ladder[None, :]
    return jnp.concatenate([jnp.sin(phases), jnp.cos(phases)], axis=1)


def turn_tables(places):
    halfway = HEAD // 2
    ladder = jnp.exp(-math.log(10000.0) * 2.0 * jnp.arange(halfway, dtype=f32) / HEAD)
    wide = jnp.tile(ladder, LOCAL_HEADS * 2)
    turned = places.astype(f32)[:, None] * wide[None, :]
    lane = jnp.arange(LOCAL_HEADS * HEAD) % HEAD
    sign = jnp.where(lane < halfway, -1.0, 1.0).astype(f32)
    return jnp.cos(turned), jnp.sin(turned) * sign[None, :]


def turn(vectors, cosine, signed_sine):
    halfway = HEAD // 2
    lane = jnp.arange(LOCAL_HEADS * HEAD) % HEAD
    from_right = jnp.concatenate([vectors[:, halfway:], vectors[:, :halfway]], axis=1)
    from_left = jnp.concatenate([vectors[:, -halfway:], vectors[:, :-halfway]], axis=1)
    partner = jnp.where((lane < halfway)[None, :], from_right, from_left)
    return vectors * cosine + partner * signed_sine


def norm_forward(values, gain_vec, bias_vec, features, time_weight):
    average = jnp.mean(values, axis=1, keepdims=True)
    centred = values - average
    inv_std = lax.rsqrt(jnp.mean(centred * centred, axis=1, keepdims=True) + norm_eps)
    normed = centred * inv_std
    scales = gain_vec.astype(f32)[None, :] + times(features, time_weight)
    return (normed * scales + bias_vec.astype(f32)[None, :], normed, scales, inv_std)


def norm_backward(grad_act, normed, scales, inv_std, one_hot):
    grad_scale = grad_act * normed
    grad_gain = jnp.sum(grad_scale, axis=0, keepdims=True)
    grad_bias = jnp.sum(grad_act, axis=0, keepdims=True)
    by_doc = contract_rows(one_hot, grad_scale.astype(bf16))
    grad_norm = grad_act * scales
    grad_input = inv_std * (
        grad_norm
        - jnp.mean(grad_norm, axis=1, keepdims=True)
        - normed * jnp.mean(grad_norm * normed, axis=1, keepdims=True)
    )
    return (grad_input, grad_gain, grad_bias, by_doc)


def lane_halves(value):
    lane = lax.broadcasted_iota(jnp.int32, value.shape, 1)
    zero = jnp.zeros_like(value)
    return jnp.where(lane < HEAD, value, zero), jnp.where(lane < HEAD, zero, value)


def dot_last(left_side, right_side):
    return lax.dot_general(
        left_side, right_side, (((1,), (1,)), ((), ())), preferred_element_type=f32
    )


def look_through(bounds, step, query_pair, kv_ref, pair, seg_q, seg_row, state):
    left, right = lane_halves(query_pair)
    lane = lax.broadcasted_iota(jnp.int32, (BLOCK_Q, LANES), 1)
    key_lanes = slice(pair * LANES, (pair + 1) * LANES)
    value_base = LOCAL_HEADS * HEAD + pair * LANES
    value_lanes = slice(value_base, value_base + LANES)

    def visit(masked):
        def body(block, carried):
            tops, totals, acc = carried
            rows = pl.ds(pl.multiple_of(block * BLOCK_K, BLOCK_K), BLOCK_K)
            keys = kv_ref[rows, key_lanes]
            values = lane_halves(kv_ref[rows, value_lanes])
            if masked:
                allowed = seg_q == seg_row(block)
            new_tops, new_totals, scales, extra = [], [], [], None
            for side, query in enumerate((left, right)):
                scores = dot_last(query, keys)
                if masked:
                    scores = jnp.where(allowed, scores, masked_value)
                top = jnp.maximum(tops[side], jnp.max(scores, axis=1, keepdims=True))
                weights = jnp.exp2(scores - top)
                scale = jnp.exp2(tops[side] - top)
                new_tops.append(top)
                new_totals.append(
                    totals[side] * scale + jnp.sum(weights, axis=1, keepdims=True)
                )
                scales.append(scale)
                part = times(weights.astype(bf16), values[side])
                extra = part if extra is None else extra + part
            acc = acc * jnp.where(lane < HEAD, scales[0], scales[1]) + extra
            return tuple(new_tops), tuple(new_totals), acc

        return body

    low, full_low, full_high, high = (bounds[k, step] for k in range(4))
    state = lax.fori_loop(low, full_low, visit(True), state)
    state = lax.fori_loop(full_low, full_high, visit(False), state)
    return lax.fori_loop(full_high, high, visit(True), state)


def pick_lane(tile, lane):
    return tile[:, lane : lane + 1]


def near_kernel(bounds, query_ref, kv_ref, seg_q_ref, seg_k_ref, acc_ref, stat_ref):
    step = pl.program_id(0)
    seg_q = seg_q_ref[...]

    def seg_row(block):
        return seg_k_ref[1:2, pl.ds(pl.multiple_of(block * BLOCK_K, BLOCK_K), BLOCK_K)]

    lane = lax.broadcasted_iota(jnp.int32, (BLOCK_Q, LANES), 1)
    stat = jnp.zeros((BLOCK_Q, LANES), f32)
    for pair in range(LOCAL_HEADS // 2):
        top = jnp.full((BLOCK_Q, 1), masked_value, f32)
        total = jnp.zeros((BLOCK_Q, 1), f32)
        acc = jnp.zeros((BLOCK_Q, LANES), f32)
        query_pair = query_ref[:, pair * LANES : (pair + 1) * LANES]
        tops, totals, acc = look_through(
            bounds, step, query_pair, kv_ref, pair, seg_q, seg_row, ((top, top), (total, total), acc)
        )
        acc_ref[:, pair * LANES : (pair + 1) * LANES] = acc
        for side in range(2):
            head = 2 * pair + side
            stat = jnp.where(lane == head, tops[side], stat)
            stat = jnp.where(lane == LOCAL_HEADS + head, totals[side], stat)
    stat_ref[...] = stat


def far_kernel(
    before, after, query_ref, prev_ref, next_ref, seg_q_ref, seg_k_ref, acc_in, stat_in, out_ref, lse_ref
):
    step = pl.program_id(0)
    seg_q = seg_q_ref[...]
    lane = lax.broadcasted_iota(jnp.int32, (BLOCK_Q, LANES), 1)
    stat = stat_in[...]
    lse_tile = jnp.zeros((BLOCK_Q, LANES), f32)
    for pair in range(LOCAL_HEADS // 2):
        lanes = slice(pair * LANES, (pair + 1) * LANES)
        tops = tuple(pick_lane(stat, 2 * pair + side) for side in range(2))
        totals = tuple(pick_lane(stat, LOCAL_HEADS + 2 * pair + side) for side in range(2))
        state = (tops, totals, acc_in[:, lanes])
        for row, bounds, kv_ref in ((0, before, prev_ref), (2, after, next_ref)):

            def seg_row(block, row=row):
                columns = pl.ds(pl.multiple_of(block * BLOCK_K, BLOCK_K), BLOCK_K)
                return seg_k_ref[row : row + 1, columns]

            state = look_through(
                bounds, step, query_ref[:, lanes], kv_ref, pair, seg_q, seg_row, state
            )
        tops, totals, acc = state
        share = jnp.where(lane < HEAD, totals[0], totals[1])
        out_ref[:, lanes] = (acc / share).astype(out_ref.dtype)
        for side in range(2):
            lse = tops[side] + jnp.log2(totals[side])
            lse_tile = jnp.where(lane == 2 * pair + side, lse, lse_tile)
    lse_ref[...] = jnp.transpose(lse_tile)[:8, :]


def attend_near(bounds, query, kv_pair, seg_q, seg_k):
    tokens, width = query.shape
    return pl.pallas_call(
        near_kernel,
        out_shape=(
            jax.ShapeDtypeStruct((tokens, width), f32),
            jax.ShapeDtypeStruct((tokens, LANES), f32),
        ),
        grid_spec=pltpu.PrefetchScalarGridSpec(
            num_scalar_prefetch=1,
            grid=(tokens // BLOCK_Q,),
            in_specs=[
                pl.BlockSpec((BLOCK_Q, width), lambda i, b: (i, 0)),
                pl.BlockSpec((tokens, 2 * width), lambda i, b: (0, 0)),
                pl.BlockSpec((BLOCK_Q, 1), lambda i, b: (i, 0)),
                pl.BlockSpec((8, tokens), lambda i, b: (0, 0)),
            ],
            out_specs=(
                pl.BlockSpec((BLOCK_Q, width), lambda i, b: (i, 0)),
                pl.BlockSpec((BLOCK_Q, LANES), lambda i, b: (i, 0)),
            ),
        ),
        name="attend_near",
    )(bounds, query, kv_pair, seg_q, seg_k)


def attend_far(before, after, query, kv_prev, kv_next, seg_q, seg_k, acc, stat):
    tokens, width = query.shape
    return pl.pallas_call(
        far_kernel,
        out_shape=(
            jax.ShapeDtypeStruct((tokens, width), bf16),
            jax.ShapeDtypeStruct((8, tokens), f32),
        ),
        grid_spec=pltpu.PrefetchScalarGridSpec(
            num_scalar_prefetch=2,
            grid=(tokens // BLOCK_Q,),
            in_specs=[
                pl.BlockSpec((BLOCK_Q, width), lambda i, b, a: (i, 0)),
                pl.BlockSpec((tokens, 2 * width), lambda i, b, a: (0, 0)),
                pl.BlockSpec((tokens, 2 * width), lambda i, b, a: (0, 0)),
                pl.BlockSpec((BLOCK_Q, 1), lambda i, b, a: (i, 0)),
                pl.BlockSpec((8, tokens), lambda i, b, a: (0, 0)),
                pl.BlockSpec((BLOCK_Q, width), lambda i, b, a: (i, 0)),
                pl.BlockSpec((BLOCK_Q, LANES), lambda i, b, a: (i, 0)),
            ],
            out_specs=(
                pl.BlockSpec((BLOCK_Q, width), lambda i, b, a: (i, 0)),
                pl.BlockSpec((8, BLOCK_Q), lambda i, b, a: (0, i)),
            ),
        ),
        name="attend_far",
    )(before, after, query, kv_prev, kv_next, seg_q, seg_k, acc, stat)


def return_kernel(
    bounds, query_ref, grad_ref, kv_ref, seg_k_ref, seg_q_ref, lse_ref, delta_ref, dq_in, dq_ref, dkv_ref
):
    step = pl.program_id(0)
    width = LOCAL_HEADS * HEAD

    @pl.when(step == 0)
    def _():
        dq_ref[...] = dq_in[...]

    seg_k = seg_k_ref[...]
    low, full_low, full_high, high = (bounds[k, step] for k in range(4))
    for pair in range(LOCAL_HEADS // 2):
        lanes = slice(pair * LANES, (pair + 1) * LANES)
        keys = lane_halves(kv_ref[:, lanes])
        values = lane_halves(kv_ref[:, width + pair * LANES : width + (pair + 1) * LANES])

        def visit(masked, pair=pair, lanes=lanes, keys=keys, values=values):
            def body(block, carried):
                dk, dv = carried
                rows = pl.ds(pl.multiple_of(block * BLOCK_Q, BLOCK_Q), BLOCK_Q)
                query_pair = query_ref[rows, lanes]
                grad_pair = grad_ref[rows, lanes]
                queries = lane_halves(query_pair)
                grads = lane_halves(grad_pair)
                if masked:
                    allowed = seg_k == seg_q_ref[0:1, rows]
                dq = None
                for side in range(2):
                    head = 2 * pair + side
                    scores = dot_last(keys[side], query_pair) - lse_ref[head : head + 1, rows]
                    if masked:
                        scores = jnp.where(allowed, scores, masked_value)
                    prob = jnp.exp2(scores)
                    grad_prob = dot_last(values[side], grad_pair) - delta_ref[head : head + 1, rows]
                    grad_scores = (prob * grad_prob).astype(bf16)
                    dv = dv + times(prob.astype(bf16), grads[side])
                    dk = dk + times(grad_scores, queries[side])
                    part = contract_rows(grad_scores, keys[side])
                    dq = part if dq is None else dq + part
                dq_ref[rows, lanes] += dq
                return dk, dv

            return body

        start = jnp.zeros((BLOCK_K, LANES), f32)
        state = lax.fori_loop(low, full_low, visit(True), (start, start))
        state = lax.fori_loop(full_low, full_high, visit(False), state)
        dk, dv = lax.fori_loop(full_high, high, visit(True), state)
        dkv_ref[:, lanes] = (dk * (1.0 / LOG2E)).astype(dkv_ref.dtype)
        dkv_ref[:, width + pair * LANES : width + (pair + 1) * LANES] = dv.astype(dkv_ref.dtype)


def attend_return(bounds, query, grad, kv_pair, seg_k, seg_q, lse, delta, dq):
    tokens, width = query.shape

    def whole(shape):
        return pl.BlockSpec(shape, lambda i, b: (0, 0))

    return pl.pallas_call(
        return_kernel,
        out_shape=(
            jax.ShapeDtypeStruct((tokens, width), f32),
            jax.ShapeDtypeStruct((tokens, 2 * width), bf16),
        ),
        grid_spec=pltpu.PrefetchScalarGridSpec(
            num_scalar_prefetch=1,
            grid=(tokens // BLOCK_K,),
            in_specs=[
                whole((tokens, width)),
                whole((tokens, width)),
                pl.BlockSpec((BLOCK_K, 2 * width), lambda i, b: (i, 0)),
                pl.BlockSpec((BLOCK_K, 1), lambda i, b: (i, 0)),
                whole((8, tokens)),
                whole((8, tokens)),
                whole((8, tokens)),
                whole((tokens, width)),
            ],
            out_specs=(
                whole((tokens, width)),
                pl.BlockSpec((BLOCK_K, 2 * width), lambda i, b: (i, 0)),
            ),
        ),
        name="attend_return",
    )(bounds, query, grad, kv_pair, seg_k, seg_q, lse, delta, dq)


def on_device(
    tokens,
    teacher,
    cotangent,
    doc_starts,
    doc_time,
    valid_mask,
    gain_one,
    bias_one,
    time_one,
    qkv_weight,
    out_weight,
    gain_two,
    bias_two,
    time_two,
    up_weight,
    up_bias,
    down_weight,
    down_bias,
):
    tok_rows = tokens.shape[1]
    width_d = tokens.shape[2]
    shards = lax.axis_size("shard")
    groups = lax.axis_size("hi")
    length = tok_rows * QUAD * groups
    quad_rows = QUAD * tok_rows
    part = LOCAL_HEADS * HEAD
    hi, lo = lax.axis_index("hi"), lax.axis_index("lo")
    core, shard = lax.axis_index("core"), lax.axis_index("shard")
    member = 2 * lo + core
    starts = doc_starts[0]
    slots = starts.shape[0]
    rows_w = qkv_weight.shape[0]

    def packed(time_weight, vectors):
        flat = jnp.concatenate([v.astype(bf16) for v in vectors])
        flat = jnp.pad(flat, (0, 16 * width_d - flat.shape[0]))
        return jnp.concatenate([time_weight, flat.reshape(16, width_d)], axis=0)

    stamp_high = (doc_time[0] // 8).astype(bf16)
    stamp_low = (doc_time[0] % 8).astype(bf16)
    pack_one = packed(time_one, [gain_one, bias_one, stamp_high, stamp_low])
    pack_two = packed(time_two, [gain_two, bias_two, down_bias, up_bias])

    def unpacked(gathered, sizes):
        blocks = gathered.reshape(shards, -1, width_d)
        time_full = blocks[:, :-16].reshape(TEMB, width_d)
        flat = blocks[:, -16:].reshape(shards, -1)
        pieces, at = [], 0
        for size in sizes:
            pieces.append(flat[:, at : at + size])
            at += size
        return time_full, pieces

    own_part = width_d // shards
    time_attn, (gain_attn, bias_attn, high_all, low_all) = unpacked(
        gather_shard(pack_one), [own_part, own_part, slots, slots]
    )
    gain_attn, bias_attn = gain_attn.reshape(-1), bias_attn.reshape(-1)
    stamps_all = high_all.astype(f32) * 8.0 + low_all.astype(f32)

    qkv_part = lax.dynamic_index_in_dim(
        qkv_weight.reshape(rows_w, 3, QUAD, part), member, 2, keepdims=False
    ).reshape(rows_w, 3 * part)
    qkv_own = gather_shard(qkv_part)

    time_mlp, (gain_mlp, bias_mlp, down_bias_full, up_bias_all) = unpacked(
        lax.all_gather(pack_two, "shard", axis=0, tiled=True),
        [own_part, own_part, own_part, up_bias.shape[0]],
    )
    gain_mlp, bias_mlp = gain_mlp.reshape(-1), bias_mlp.reshape(-1)
    down_bias_full = down_bias_full.reshape(-1)
    hidden_half = up_bias.shape[0] // 2
    up_bias_own = lax.dynamic_index_in_dim(
        up_bias_all.reshape(shards, 2, hidden_half), core, 1, keepdims=False
    ).reshape(-1)
    if shards == 2:
        out_own = lax.all_gather(half_of(out_weight, core), "shard", axis=0, tiled=True)
    else:
        out_all = lax.all_gather(out_weight, "shard", axis=0, tiled=True)
        out_own = lax.dynamic_index_in_dim(
            out_all.reshape(2, 2, part, width_d), core, 1, keepdims=False
        ).reshape(2 * part, width_d)
    up_part = lax.dynamic_index_in_dim(
        up_weight.reshape(rows_w, shards, 2, hidden_half), core, 2, keepdims=False
    ).reshape(rows_w, shards * hidden_half)
    up_own = lax.all_gather(up_part, "shard", axis=0, tiled=True)
    down_own = lax.all_gather(half_of(down_weight, core), "shard", axis=0, tiled=True)

    block_base = (hi * QUAD + member) * tok_rows
    quad_base = hi * quad_rows
    own_seg = segments_at(starts, block_base + jnp.arange(tok_rows, dtype=jnp.int32))
    one_hot = (own_seg[:, None] == jnp.arange(slots, dtype=jnp.int32)[None, :]).astype(bf16)
    features_all = time_features(stamps_all.reshape(-1)).astype(bf16).reshape(shards, slots, TEMB)
    features_docs = time_features(doc_time[0]).astype(bf16)
    features = times(one_hot, features_docs).astype(bf16)
    quad_places = quad_base + jnp.arange(quad_rows, dtype=jnp.int32)
    quad_seg = segments_at(starts, quad_places)
    offsets = quad_places - begins_at(starts, quad_places)
    cosine, signed_sine = turn_tables(offsets)
    seg_rows = jnp.concatenate(
        [
            segments_at(starts, quad_places - quad_rows)[None],
            quad_seg[None],
            segments_at(starts, quad_places + quad_rows)[None],
            jnp.zeros((5, quad_rows), jnp.int32),
        ],
        axis=0,
    )
    seg_columns = [seg_rows[k][:, None] for k in range(3)]

    valid = valid_mask[0].astype(f32)
    counted = jnp.full((8, LANES), jnp.sum(valid))
    for axis in ("core", "lo", "hi", "shard"):
        counted = sum_all(counted, axis)
    counted = counted[0, 0]

    block_in = tokens[0].astype(f32)
    act_pre, normed_one, scales_one, inv_one = norm_forward(
        block_in, gain_attn, bias_attn, features, time_attn
    )
    act_one = act_pre.astype(bf16)
    act_far = flip(act_one, "lo")
    act_pair = in_order(core, act_one, flip(act_one, "core"), 0)
    act_far = in_order(core, act_far, flip(act_far, "core"), 0)
    act_quad = in_order(lo, act_pair, act_far, 0)
    joined = times(act_quad, qkv_own)
    key_low = turn(joined[:, part : 2 * part], cosine, signed_sine).astype(bf16)
    kv_pair = jnp.concatenate([key_low, joined[:, 2 * part :].astype(bf16)], axis=1)
    up_pairs = [(i, i + 1) for i in range(groups - 1)]
    down_pairs = [(i + 1, i) for i in range(groups - 1)]
    kv_prev = lax.ppermute(kv_pair, "hi", up_pairs)
    kv_next = lax.ppermute(kv_pair, "hi", down_pairs)
    query_low = (turn(joined[:, :part], cosine, signed_sine) * (LOG2E * HEAD**-0.5)).astype(bf16)

    def ranges(row_shift, row_block, col_shift, col_block):
        return block_ranges(
            starts,
            length,
            quad_base + row_shift,
            row_block,
            quad_base + col_shift,
            col_block,
            quad_rows,
        )

    acc, stat = attend_near(
        ranges(0, BLOCK_Q, 0, BLOCK_K), query_low, kv_pair, seg_columns[1], seg_rows
    )
    mixed_quad, lse = attend_far(
        ranges(0, BLOCK_Q, -quad_rows, BLOCK_K),
        ranges(0, BLOCK_Q, quad_rows, BLOCK_K),
        query_low,
        kv_prev,
        kv_next,
        seg_columns[1],
        seg_rows,
        acc,
        stat,
    )

    def to_chip(value):
        kept, sent = half_of(value, lo), half_of(value, 1 - lo)
        return in_order(lo, kept, flip(sent, "lo"), 1)

    def to_quad(value):
        left, right = value[:, :part], value[:, part:]
        kept = jnp.where(lo == 0, left, right)
        sent = jnp.where(lo == 0, right, left)
        return in_order(lo, kept, flip(sent, "lo"), 0)

    def both_cores(value):
        return in_order(core, value, flip(value, "core"), 0)

    def own_tokens(partial):
        sent = flip(half_of(partial, 1 - core).astype(bf16), "core")
        return half_of(partial, core) + sent.astype(f32)

    mixed_low = to_chip(mixed_quad)
    middle = block_in + own_tokens(times(mixed_low, out_own))

    act_pre_two, normed_two, scales_two, inv_two = norm_forward(
        middle, gain_mlp, bias_mlp, features, time_mlp
    )
    act_two = both_cores(act_pre_two.astype(bf16))
    upper_in = times(act_two, up_own) + up_bias_own.astype(f32)[None, :]
    normal_cdf = 0.5 + 0.5 * lax.erf(upper_in * math.sqrt(0.5))
    density = jnp.exp(-0.5 * upper_in * upper_in) * (1.0 / math.sqrt(2.0 * math.pi))
    hidden = (upper_in * normal_cdf).astype(bf16)
    slope = (normal_cdf + upper_in * density).astype(bf16)
    block_out = (
        middle + own_tokens(times(hidden, down_own)) + down_bias_full.astype(f32)[None, :]
    )
    misfit = block_out - teacher[0].astype(f32)
    square_sum = jnp.sum(valid[:, None] * misfit * misfit)
    grad_final = (
        cotangent[0].astype(f32) + 2.0 / (counted * width_d) * valid[:, None] * misfit
    )
    grad_mid_own = grad_final.astype(bf16)
    grad_mid = both_cores(grad_mid_own)
    grad_down = contract_rows(hidden, grad_mid)
    grad_down_bias = jnp.sum(grad_mid_own.astype(f32), axis=0, keepdims=True)
    grad_upper = (times_trans(grad_mid, down_own) * slope.astype(f32)).astype(bf16)
    grad_up = contract_rows(act_two, grad_upper)
    grad_up_bias = jnp.sum(grad_upper.astype(f32), axis=0)
    grad_act_two = own_tokens(times_trans(grad_upper, up_own))
    grad_in_two, grad_gain_two, grad_bias_two, by_doc_two = norm_backward(
        grad_act_two, normed_two, scales_two, inv_two, one_hot
    )
    grad_middle = grad_final + grad_in_two
    grad_branch = both_cores(grad_middle.astype(bf16))
    grad_mixed = times_trans(grad_branch, out_own).astype(bf16)
    grad_out = contract_rows(mixed_low, grad_branch)

    if shards == 2:
        out_rows = grad_out
    else:
        by_core = lax.all_gather(grad_out.astype(bf16), "core", axis=0, tiled=False)
        out_rows = jnp.transpose(
            by_core.reshape(2, 2, part, width_d), (1, 0, 2, 3)
        ).reshape(2 * 2 * part, width_d)
    blocks = [
        grad_down.astype(bf16).reshape(shards, -1, width_d),
        grad_up.astype(bf16).reshape(shards, -1, width_d),
        out_rows.astype(bf16).reshape(shards, -1, width_d),
    ]
    sizes = [b.shape[1] for b in blocks]
    pairs = 2 * groups
    pieces = jnp.concatenate(
        [b.reshape(shards, pairs, -1, width_d) for b in blocks], axis=2
    ).reshape(-1, width_d)
    reduced = lax.psum_scatter(pieces, ("shard", "hi", "lo"), scatter_dimension=0, tiled=True)
    everyone = lax.all_gather(reduced, ("hi", "lo", "core"), axis=0, tiled=True)
    everyone = everyone.reshape(pairs, 2, -1, width_d)
    cut = [0]
    for size in sizes:
        cut.append(cut[-1] + size // pairs)

    def of_block(k):
        return jnp.transpose(everyone[:, :, cut[k] : cut[k + 1]], (1, 0, 2, 3)).reshape(
            2, sizes[k], width_d
        )

    down_total = of_block(0).reshape(2 * sizes[0], width_d).astype(f32)
    up_total = (
        jnp.transpose(of_block(1).reshape(2, rows_w, shards, hidden_half), (1, 2, 0, 3))
        .reshape(rows_w, shards * 2 * hidden_half)
        .astype(f32)
    )
    if shards == 2:
        out_total = of_block(2).reshape(2 * sizes[2], width_d).astype(f32)
    else:
        out_total = of_block(2)[0].astype(f32)

    grad_quad = to_quad(grad_mixed)
    head_of = jnp.arange(part, dtype=jnp.int32) // HEAD
    summing = (jnp.arange(8, dtype=jnp.int32)[:, None] == head_of[None, :]).astype(f32)
    delta = lax.dot_general(
        summing,
        grad_quad.astype(f32) * mixed_quad.astype(f32),
        (((1,), (1,)), ((), ())),
        precision=lax.Precision.HIGHEST,
        preferred_element_type=f32,
    )
    seg_q_rows = jnp.broadcast_to(quad_seg[None], (8, quad_rows))

    def give_back(row_shift, kv, k, dq):
        return attend_return(
            ranges(row_shift, BLOCK_K, 0, BLOCK_Q),
            query_low,
            grad_quad,
            kv,
            seg_columns[k],
            seg_q_rows,
            lse,
            delta,
            dq,
        )

    dq, dkv_prev = give_back(-quad_rows, kv_prev, 0, jnp.zeros((quad_rows, part), f32))
    from_next = lax.ppermute(dkv_prev, "hi", down_pairs)
    dq, dkv_next = give_back(quad_rows, kv_next, 2, dq)
    from_prev = lax.ppermute(dkv_next, "hi", up_pairs)
    dq, dkv_own = give_back(0, kv_pair, 1, dq)
    dkv = dkv_own.astype(f32) + from_next.astype(f32) + from_prev.astype(f32)
    grad_joined = jnp.concatenate(
        [
            turn(dq * HEAD**-0.5, cosine, -signed_sine),
            turn(dkv[:, :part], cosine, -signed_sine),
            dkv[:, part:],
        ],
        axis=1,
    ).astype(bf16)

    partial_act = times_trans(grad_joined, qkv_own)
    far_act = flip(half_of(partial_act, 1 - lo).astype(bf16), "lo")
    grad_act_one = own_tokens(half_of(partial_act, lo) + far_act.astype(f32))
    grad_qkv = contract_rows(act_quad, grad_joined)
    grad_in_one, grad_gain_one, grad_bias_one, by_doc_one = norm_backward(
        grad_act_one, normed_one, scales_one, inv_one, one_hot
    )
    input_grad = grad_middle + grad_in_one

    qkv_rows = scatter_sum(scatter_sum(grad_qkv, "shard"), "hi").astype(bf16)
    qkv_rows = gather_back(qkv_rows, "hi").reshape(1, rows_w, 3 * part)
    qkv_rows = gather_back(gather_back(qkv_rows, "core"), "lo")
    qkv_total = (
        jnp.transpose(qkv_rows.reshape(QUAD, rows_w, 3, part), (1, 2, 0, 3))
        .reshape(rows_w, 3 * QUAD * part)
        .astype(f32)
    )

    bias_slots = jnp.where(
        jnp.arange(2, dtype=jnp.int32)[None, :, None] == core,
        grad_up_bias.reshape(shards, 1, hidden_half),
        0.0,
    ).reshape(-1, width_d)
    summed_rows = [grad_gain_one, grad_bias_one, grad_gain_two, grad_bias_two, grad_down_bias]
    small = jnp.concatenate(
        summed_rows + [bias_slots, jnp.full((1, width_d), square_sum), by_doc_one, by_doc_two],
        axis=0,
    )
    filled = small.shape[0]
    small = jnp.pad(small, ((0, -filled % 8), (0, 0)))
    for axis in ("hi", "lo", "core"):
        small = sum_all(small, axis)
    small_all = gather_shard(small).reshape(shards, -1, width_d)
    bias_rows = bias_slots.shape[0]
    head_rows = 6 + bias_rows
    totals = jnp.sum(small_all[:, :head_rows], axis=0)
    docs_one = small_all[:, head_rows : head_rows + slots]
    docs_two = small_all[:, head_rows + slots : head_rows + 2 * slots]

    def own_vector(row):
        return lax.dynamic_slice_in_dim(row, shard * own_part, own_part, 0)

    own_features = lax.dynamic_slice_in_dim(
        features_all, shard * (TEMB // shards), TEMB // shards, 2
    ).astype(f32)

    def time_total(docs):
        return lax.dot_general(
            own_features,
            docs,
            (((0, 1), (0, 1)), ((), ())),
            precision=lax.Precision.HIGHEST,
            preferred_element_type=f32,
        )

    up_bias_total = lax.dynamic_slice_in_dim(
        totals[5 : 5 + bias_rows].reshape(-1), shard * 2 * hidden_half, 2 * hidden_half, 0
    )
    loss_value = totals[5 + bias_rows, 0] / (counted * width_d)
    return (
        block_out.astype(bf16)[None],
        loss_value,
        input_grad[None],
        own_vector(totals[0]),
        own_vector(totals[1]),
        time_total(docs_one),
        qkv_total,
        out_total,
        own_vector(totals[2]),
        own_vector(totals[3]),
        time_total(docs_two),
        up_total,
        up_bias_total,
        down_total,
        own_vector(totals[4]),
    )


def solution(mesh):
    ctx, shards = mesh.shape["ctx"], mesh.shape["shard"]
    fine = Mesh(
        mesh.devices.reshape(ctx // QUAD, 2, 2, shards), ("hi", "lo", "core", "shard")
    )
    blocks = ("hi", "lo", "core")
    in_specs = (
        P("shard", blocks, None),
        P("shard", blocks, None),
        P("shard", blocks, None),
        P("shard", None),
        P("shard", None),
        P("shard", blocks),
        P("shard"),
        P("shard"),
        P("shard", None),
        P("shard", None),
        P("shard", None),
        P("shard"),
        P("shard"),
        P("shard", None),
        P("shard", None),
        P("shard"),
        P("shard", None),
        P("shard"),
    )
    out_specs = (
        P("shard", blocks, None),
        P(),
        P("shard", blocks, None),
        P("shard"),
        P("shard"),
        P("shard", None),
        P("shard", None),
        P("shard", None),
        P("shard"),
        P("shard"),
        P("shard", None),
        P("shard", None),
        P("shard"),
        P("shard", None),
        P("shard"),
    )
    return jax.shard_map(
        on_device, mesh=fine, in_specs=in_specs, out_specs=out_specs, check_vma=False
    )
```

time: 1910 us -> 970 us (0.51)
  waiting for transfers between devices: 869 us -> 352 us
  blocking collectives: 229 us -> 10.5 us
  Pallas kernels: 0 us -> 213 us
  matrix products: 255 us -> 87 us
  starting transfers between devices: 212 us -> 46.1 us
  local copies, waits for them, and re-layouts: 183 us -> 131 us
  between operations: 39.4 us -> 18.2 us
    pallas_call x0 -> x5, Pallas kernels: none -> 213 us  [the longest x3 120 us: attend_return(): pl.pallas_call(return_kernel, out_shape=(jax.ShapeDtypeStruct((tokens, wi...]
    psum x1 -> x0, waiting for transfers between devices: 198 us -> none  [on_device(): lax.psum(attn_time.astype(jnp.bfloat16), 'ctx').astype(jnp.float32)]
    psum x2 -> x0, blocking collectives: 170 us -> none  [the longest x1 134 us: on_device(): lax.psum((jnp.sum(weight_mask[:, None] * misfit * misfit), jnp.sum(weight...]
    ppermute x16 -> x36, waiting for transfers between devices: 311 us -> 144 us  [the longest x16 58.6 us: flip(): return lax.ppermute(value, axis, [(0, 1), (1, 0)])]
    ppermute x16 -> x36, starting transfers between devices: 211 us -> 45.4 us  [the longest x1 13.6 us: on_device(): from_prev = lax.ppermute(dkv_next, 'hi', up_pairs)]
    dot_general x33 -> x16, matrix products: 217 us -> 60.8 us  [the longest x7 33.7 us: times(): return jnp.dot(left_side, right_side, preferred_element_type=f32)]
    reduce_scatter x6 -> x1, waiting for transfers between devices: 299 us -> 171 us  [on_device(): lax.psum_scatter(pieces, ('shard', 'hi', 'lo'), scatter_dimension=0, tile...]
    convert_element_type x3 -> x14, local copies, waits for them, and re-layouts: 8.79 us -> 57.4 us  [the longest x2 27.2 us: on_device(): up_total = jnp.transpose(of_block(1).reshape(2, rows_w, shards, hidden_ha...]
  transfers between devices with their start and end apart: 27 -> 41, of which waited for: 12 -> 23; matrix products, arithmetic and copies ran while one was open for 13% -> 21% of each run, Pallas kernels for 0% -> 22%
where the time goes in v1:
time: 970 us; the launch traced here: 954 us
  waiting for transfers between devices  352 us (36%)
  Pallas kernels  213 us (22%)
  local copies, waits for them, and re-layouts  131 us (14%)
  other arithmetic  95.7 us (10%)
  matrix products  87 us (9%)
  starting transfers between devices  46.1 us (5%)
  between operations  18.2 us (2%)
  blocking collectives  10.5 us (1%)
    reduce_scatter x1, waiting for transfers between devices, on_device(): lax.psum_scatter(pieces, ('shard', 'hi', 'lo'), scatter_dimension=0, tile...  171 us
    pallas_call x3, Pallas kernels, attend_return(): pl.pallas_call(return_kernel, out_shape=(jax.ShapeDtypeStruct((tokens, wi...  120 us
    pallas_call x1, Pallas kernels, attend_near(): pl.pallas_call(near_kernel, out_shape=(jax.ShapeDtypeStruct((tokens, widt...  75.9 us
    ppermute x16, waiting for transfers between devices, flip(): return lax.ppermute(value, axis, [(0, 1), (1, 0)])  58.6 us
    ppermute x9, waiting for transfers between devices, sum_all(): value = value + lax.ppermute(value, axis, xor_pairs(size, bit))  52.7 us
    all_gather x1, waiting for transfers between devices, on_device(): lax.all_gather(half_of(down_weight, core), 'shard', axis=0, tiled=True)  37.2 us
    dot_general x7, matrix products, times(): return jnp.dot(left_side, right_side, preferred_element_type=f32)  33.7 us
    unnamed x181, local copies, waits for them, and re-layouts  32.4 us
  transfers between devices with their start and end apart: 41, of which 23 were waited for; matrix products, arithmetic and copies ran while one was open for 21% of the time, Pallas kernels for 22%

profile of v1, /device:TPU:0, one launch (start us, length us, event | category | flops | bytes accessed | tf_op | source)
XLA Modules:
  0.0 953.8 jit_solution(6031982799273873410)
XLA Ops:
  16.7 7.2 collective-permute-done
  28.0 4.6 copy.85
  37.2 6.4 copy.99
  54.4 3.5 maximum_select_fusion.3
  57.9 6.4 fusion.54
  69.2 11.1 %fusion.29 = (bf16[2048,256]{1,0:T(8,128)(2,1)S(1)}, bf16[2048,256]{1,0:T(8,128)(2,1)}) fusion(f32[2048,768]{1,0:T(8,128)S(1)} %fusion.54, f32[2048,32]{1,0:T(8,128)S(1)} %get-tuple-element.84, f32[2048,224]{1,0:T(8,128)S(1)} %get-tuple-element.88, f32[2048,224]{1,0:T(8,128)S(1)} %get-tuple-element.87, f32[2048,32]{1,0:T(8,128)S(1)} %get-tuple-element.83, ...), kind=kLoop, calls=%fused_computation.51 | loop fusion | flops 8912896 | bytes 14690560 | tf_op jit(solution)/shard_map/convert_element_type | solution.py:561
  80.5 4.7 collective-permute-start.5
  89.6 75.9 %attend_near.1 = (f32[2048,256]{1,0:T(8,128)}, f32[2048,128]{1,0:T(8,128)}) custom-call(s32[4,8]{1,0:T(4,128)} %pad_add_fusion.2.bounds, bf16[2048,256]{1,0:T(8,128)(2,1)} %get-tuple-element.80.query_ref, bf16[2048,512]{1,0:T(8,128)(2,1)} %copy-done.9, s32[2048,1]{1,0:T(8,128)} %copy.98.seg_q_ref.seg_k_ref, s32[8,2048]{1,0:T(8,128)} %add_add_fusion.1.seg_k_ref), custom_call_target="tpu_custom_call" | custom-call | tf_op jit(solution)/shard_map/attend_near/pallas_call | solution.py:294
  165.5 16.6 %attend_far.1 = (bf16[2048,256]{1,0:T(8,128)(2,1)}, f32[8,2048]{1,0:T(8,128)}) custom-call(s32[4,8]{1,0:T(4,128)} %get-tuple-element.150.before, s32[4,8]{1,0:T(4,128)} %get-tuple-element.151.after, bf16[2048,256]{1,0:T(8,128)(2,1)} %get-tuple-element.80.query_ref, bf16[2048,512]{1,0:T(8,128)(2,1)} %collective-permute-done.5.prev_ref.kv_ref, ...), custom_call_target="tpu_custom_call" | custom-call | tf_op jit(solution)/shard_map/attend_far/pallas_call | solution.py:320
  185.0 12.6 %collective-permute-done.7 = bf16[1024,256]{1,0:T(8,128)(2,1)S(1)} collective-permute-done((bf16[1024,256]{1,0:T(8,128)(2,1)S(1)}, bf16[1024,256]{1,0:T(8,128)(2,1)S(1)}, u32[]{:S(2)}, u32[]{:S(2)}) %collective-permute-start.7) | collective-permute-done | bytes 524320 | tf_op jit(solution)/shard_map/ppermute | solution.py:27
  205.1 10.5 %all_gather.16 = bf16[288,1024]{1,0:T(8,128)(2,1)S(1)} all-gather(bf16[144,1024]{1,0:T(8,128)(2,1)S(1)} %pad_maximum_fusion.6), channel_id=1, replica_groups=mesh['hi'=4,'lo'=2,'core'=2,'shard'=2] {'shard'}, dimensions={0}, use_global_device_ids=true | all-gather | bytes 884736 | tf_op jit(solution)/shard_map/all_gather | solution.py:501
  224.9 12.7 %multiply_convert_fusion.1 = (bf16[1024,2048]{1,0:T(8,128)(2,1)}, f32[1024,2048]{1,0:T(8,128)}) fusion(f32[2048]{0:T(1024)S(1)} %bitcast.561, bf16[1024,2048]{0,1:T(8,128)(2,1)} %all-gather.7.cloned.1.call-done, bf16[512,1024]{1,0:T(8,128)(2,1)S(1)} %collective-permute-done.9, bf16[512,1024]{1,0:T(8,128)(2,1)} %get-tuple-element.144, pred[]{:T(512)S(6)} %eq.157), kind=kOutput, calls=%fused_computation.11 | convolution fusion | flops 4316987392 | bytes 18882560 | tf_op jit(solution)/shard_map/dot_general | solution.py:96
  237.6 37.2 %all-gather.9.cloned.1.call-done = bf16[2048,1024]{1,0:T(8,128)(2,1)} async-done(((bf16[1024,1024]{1,0:T(8,128)(2,1)}), bf16[2048,1024]{1,0:T(8,128)(2,1)}) %all-gather.9.cloned.1.call-update) | async-done | bytes 4194320 | tf_op jit(solution)/shard_map/all_gather | solution.py:521
  274.8 7.5 fusion.136
  309.3 13.0 %convert_reduce_fusion = (f32[2048]{0:T(1024)}, bf16[1024,2048]{1,0:T(8,128)(2,1)}) fusion(f32[1024,2048]{1,0:T(8,128)} %get-tuple-element.147, f32[2048]{0:T(1024)S(1)} %bitcast.562, bf16[2048,1024]{1,0:T(8,128)(2,1)S(1)} %copy-done.73, bf16[512,1024]{1,0:T(8,128)(2,1)S(1)} %collective-permute-done.16, bf16[512,1024]{1,0:T(8,128)(2,1)S(1)} %get-tuple-element.64, ...), kind=kOutput, calls=%fused_computation.9 | convolution fusion | flops 4335859712 | bytes 18890752 | tf_op jit(solution)/shard_map/dot_general | solution.py:90
  322.4 6.5 fusion.137
  332.5 8.5 convolution_convert_fusion
  341.0 7.1 reshape_reshape.13
  348.1 5.4 fusion.124
  357.8 5.0 convolution_convert_fusion.1
  365.0 4.0 pad_maximum_fusion
  369.2 171.1 %reduce-scatter.2.cloned.1.call-done = bf16[288,1024]{1,0:T(8,128)(2,1)} async-done(((bf16[4608,1024]{1,0:T(8,128)(2,1)}), bf16[288,1024]{1,0:T(8,128)(2,1)}) %reduce-scatter.2.cloned.1.call-update) | async-done | bytes 589840 | tf_op jit(solution)/shard_map/reduce_scatter | solution.py:665
  546.6 16.7 %collective-permute-done.19 = bf16[1024,256]{1,0:T(8,128)(2,1)S(1)} collective-permute-done((bf16[1024,256]{1,0:T(8,128)(2,1)S(1)}, bf16[1024,256]{1,0:T(8,128)(2,1)S(1)}, u32[]{:S(2)}, u32[]{:S(2)}) %collective-permute-start.19) | collective-permute-done | bytes 524320 | tf_op jit(solution)/shard_map/ppermute | solution.py:27
  567.6 9.9 %attend_return.3 = (f32[2048,256]{1,0:T(8,128)}, bf16[2048,512]{1,0:T(8,128)(2,1)}) custom-call(s32[4,8]{1,0:T(4,128)} %get-tuple-element.153.bounds, bf16[2048,256]{1,0:T(8,128)(2,1)} %get-tuple-element.80.query_ref, bf16[2048,256]{1,0:T(8,128)(2,1)} %copy-done.4, bf16[2048,512]{1,0:T(8,128)(2,1)} %collective-permute-done.5.prev_ref.kv_ref, ...), custom_call_target="tpu_custom_call" | custom-call | tf_op jit(solution)/shard_map/attend_return/pallas_call | solution.py:406
  577.5 10.7 %attend_return.4 = (f32[2048,256]{1,0:T(8,128)}, bf16[2048,512]{1,0:T(8,128)(2,1)}) custom-call(s32[4,8]{1,0:T(4,128)} %get-tuple-element.152.bounds, bf16[2048,256]{1,0:T(8,128)(2,1)} %get-tuple-element.80.query_ref, bf16[2048,256]{1,0:T(8,128)(2,1)} %copy-done.4, bf16[2048,512]{1,0:T(8,128)(2,1)} %collective-permute-done.6.next_ref.kv_ref, ...), custom_call_target="tpu_custom_call" | custom-call | tf_op jit(solution)/shard_map/attend_return/pallas_call | solution.py:406
  588.2 13.6 %collective-permute-start.21 = (bf16[2048,512]{1,0:T(8,128)(2,1)}, bf16[2048,512]{1,0:T(8,128)(2,1)S(1)}, u32[]{:S(2)}, u32[]{:S(2)}) collective-permute-start(bf16[2048,512]{1,0:T(8,128)(2,1)} %get-tuple-element.34), channel_id=1, source_target_pairs={{0,8},{8,16},{16,24},{1,9},{9,17},{17,25},{2,10},{10,18},{18,26},{... | collective-permute-start | bytes 6291464 | tf_op jit(solution)/shard_map/ppermute | solution.py:716
  603.1 99.8 %attend_return.5 = (f32[2048,256]{1,0:T(8,128)}, bf16[2048,512]{1,0:T(8,128)(2,1)}) custom-call(s32[4,8]{1,0:T(4,128)} %pad_add_fusion.2.bounds, bf16[2048,256]{1,0:T(8,128)(2,1)} %get-tuple-element.80.query_ref, bf16[2048,256]{1,0:T(8,128)(2,1)} %copy-done.4, bf16[2048,512]{1,0:T(8,128)(2,1)} %copy-done.9, s32[2048,1]{1,0:T(8,128)} %copy.98.seg_q_ref.seg_k_ref, ...), custom_call_target="tpu_custom_call" | custom-call | tf_op jit(solution)/shard_map/attend_return/pallas_call | solution.py:406
  711.0 10.7 %fusion.31 = (bf16[2048,256]{1,0:T(8,128)(2,1)S(1)}, bf16[2048,256]{1,0:T(8,128)(2,1)S(1)}) fusion(f32[2048,32]{1,0:T(8,128)S(1)} %get-tuple-element.97, f32[2048,224]{1,0:T(8,128)S(1)} %get-tuple-element.99, f32[2048,224]{1,0:T(8,128)S(1)} %get-tuple-element.98, f32[2048,32]{1,0:T(8,128)S(1)} %get-tuple-element.96, f32[256]{0:T(256)S(1)} %broadcast_select_fusion.3, ...), kind=kLoop, calls=%fused_computation.53 | loop fusion | flops 9437184 | bytes 14690560 | tf_op jit(solution)/shard_map/convert.20
  721.7 5.4 fusion.47
  727.1 3.4 copy-done.16
  734.5 3.7 fusion.46
  740.1 13.6 %collective-permute-done.29 = bf16[512,768]{0,1:T(8,128)(2,1)S(1)} collective-permute-done((bf16[512,768]{0,1:T(8,128)(2,1)S(1)}, bf16[512,768]{0,1:T(8,128)(2,1)S(1)}, u32[]{:S(2)}, u32[]{:S(2)}) %collective-permute-start.29) | collective-permute-done | bytes 786464 | tf_op jit(solution)/shard_map/ppermute | solution.py:56
  756.9 8.4 collective-permute-done.30
  765.5 9.5 collective-permute-done.22
  775.0 3.5 convert_add_fusion
  786.6 3.4 collective-permute-done.32
  793.9 7.0 collective-permute-done.33
  802.1 5.0 fusion.121
  811.4 6.7 collective-permute-done.24
  824.4 5.1 collective-permute-done.25
  831.4 29.5 %collective-permute-done.26 = f32[48,1024]{1,0:T(8,128)S(1)} collective-permute-done((f32[48,1024]{1,0:T(8,128)S(1)}, f32[48,1024]{1,0:T(8,128)S(1)}, u32[]{:S(2)}, u32[]{:S(2)}) %collective-permute-start.26) | collective-permute-done | bytes 196640 | tf_op jit(solution)/shard_map/ppermute | solution.py:73
  864.5 4.9 collective-permute-done.28
  879.6 7.6 copy.103
  887.2 8.2 reshape.2035
  896.9 11.8 %convert_bitcast_fusion.1 = (f32[2,8,128,1024]{3,2,0,1:T(8,128)}, f32[2,8,128,1024]{3,2,0,1:T(8,128)}) fusion(bf16[8,2,288,1024]{3,2,1,0:T(8,128)(2,1)} %bitcast.513), kind=kLoop, calls=%fused_computation.8 | loop fusion | flops 4194304 | bytes 25165824 | tf_op jit(solution)/shard_map/convert_element_type | solution.py:677
  910.2 15.4 %copy.105 = f32[2,8,128,1024]{3,0,2,1:T(2,128)} copy(f32[2,8,128,1024]{3,2,0,1:T(8,128)} %get-tuple-element.75) | data formatting | bytes 16777216 | tf_op jit(solution)/shard_map/convert_element_type | solution.py:681
  925.6 11.8 %reshape.2037 = f32[512,4096]{1,0:T(8,128)} reshape(f32[512,2,2,1024]{3,2,1,0:T(2,128)} %bitcast.511) | data formatting | bytes 16777216 | tf_op jit(solution)/shard_map/convert_element_type | solution.py:681
  937.4 8.5 copy.106
  (408 shorter events, 164.3 us)
Async XLA Ops:
  7.2 177.7 %all-gather.5.cloned.1.call-start = ((), (), s32[]{:S(2)}) async-start(), calls=%async_computation.1 | async-start | bytes 1572864 | tf_op jit(solution)/shard_map/all_gather | solution.py:511
  9.3 212.8 %all-gather.7.cloned.1.call-start = ((), (), s32[]{:S(2)}) async-start(), calls=%async_computation.2 | async-start | bytes 6291456 | tf_op jit(solution)/shard_map/all_gather | solution.py:520
  12.5 11.5 %collective-permute-start = (bf16[144,1024]{1,0:T(8,128)(2,1)S(1)}, bf16[144,1024]{1,0:T(8,128)(2,1)S(1)}, u32[]{:S(2)}, u32[]{:S(2)}) collective-permute-start(bf16[144,1024]{1,0:T(8,128)(2,1)S(1)} %pad_maximum_fusion.5), channel_id=1, source_target_pairs={{0,1},{1,0},{2,3},{3,2},{4,5},{5,4},{6,7},{7,6},{8,9},{9,8},{10,11... | collective-permute-start | bytes 884744 | tf_op jit(solution)/shard_map/ppermute | solution.py:27
  26.8 23.0 %collective-permute-start.2 = (bf16[512,1024]{1,0:T(8,128)(2,1)S(1)}, bf16[512,1024]{1,0:T(8,128)(2,1)S(1)}, u32[]{:S(2)}, u32[]{:S(2)}) collective-permute-start(bf16[512,1024]{1,0:T(8,128)(2,1)S(1)} %get-tuple-element.142), channel_id=1, source_target_pairs={{0,4},{4,0},{1,5},{5,1},{2,6},{6,2},{3,7},{7,3},{8,12},{12,8},{9,1... | collective-permute-start | bytes 3145736 | tf_op jit(solution)/shard_map/ppermute | solution.py:27
  34.8 23.1 %collective-permute-start.4 = (bf16[512,768]{0,1:T(8,128)(2,1)}, bf16[512,768]{0,1:T(8,128)(2,1)}, u32[]{:S(2)}, u32[]{:S(2)}) collective-permute-start(bf16[512,768]{0,1:T(8,128)(2,1)} %bitcast.11), channel_id=1, source_target_pairs={{0,1},{1,0},{2,3},{3,2},{4,5},{5,4},{6,7},{7,6},{8,9},{9,8},{10,11... | collective-permute-start | bytes 2359304 | tf_op jit(solution)/shard_map/ppermute | solution.py:27
  46.7 228.1 %all-gather.9.cloned.1.call-start = ((), (), s32[]{:S(2)}) async-start(), calls=%async_computation.3 | async-start | bytes 6291456 | tf_op jit(solution)/shard_map/all_gather | solution.py:521
  47.3 4.3 collective-permute-start.1
  49.7 4.6 collective-permute-start.3
  80.5 85.0 %collective-permute-start.5 = (bf16[2048,512]{1,0:T(8,128)(2,1)S(1)}, bf16[2048,512]{1,0:T(8,128)(2,1)}, u32[]{:S(2)}, u32[]{:S(2)}) collective-permute-start(bf16[2048,512]{1,0:T(8,128)(2,1)S(1)} %pad_maximum_fusion.2.kv_ref), channel_id=1, source_target_pairs={{0,8},{8,16},{16,24},{1,9},{9,17},{17,25},{2,10},{10,18},{18,26},{... | collective-permute-start | bytes 6291464 | tf_op jit(solution)/shard_map/ppermute | solution.py:565
  85.2 80.3 %collective-permute-start.6 = (bf16[2048,512]{1,0:T(8,128)(2,1)S(1)}, bf16[2048,512]{1,0:T(8,128)(2,1)}, u32[]{:S(2)}, u32[]{:S(2)}) collective-permute-start(bf16[2048,512]{1,0:T(8,128)(2,1)S(1)} %pad_maximum_fusion.2.kv_ref), channel_id=1, source_target_pairs={{8,0},{16,8},{24,16},{9,1},{17,9},{25,17},{10,2},{18,10},{26,18},{... | collective-permute-start | bytes 6291464 | tf_op jit(solution)/shard_map/ppermute | solution.py:566
  183.4 14.1 %collective-permute-start.7 = (bf16[1024,256]{1,0:T(8,128)(2,1)S(1)}, bf16[1024,256]{1,0:T(8,128)(2,1)S(1)}, u32[]{:S(2)}, u32[]{:S(2)}) collective-permute-start(bf16[1024,256]{1,0:T(8,128)(2,1)S(1)} %get-tuple-element.104), channel_id=1, source_target_pairs={{0,4},{4,0},{1,5},{5,1},{2,6},{6,2},{3,7},{7,3},{8,12},{12,8},{9,1... | collective-permute-start | bytes 1572872 | tf_op jit(solution)/shard_map/ppermute | solution.py:27
  202.4 14.0 %collective-permute-start.8 = (bf16[512,1024]{1,0:T(8,128)(2,1)S(1)}, bf16[512,1024]{1,0:T(8,128)(2,1)}, u32[]{:S(2)}, u32[]{:S(2)}) collective-permute-start(bf16[512,1024]{1,0:T(8,128)(2,1)S(1)} %dynamic-slice_convert_fusion.4), channel_id=1, source_target_pairs={{0,2},{2,0},{1,3},{3,1},{4,6},{6,4},{5,7},{7,5},{8,10},{10,8},{9,1... | collective-permute-start | bytes 3145736 | tf_op jit(solution)/shard_map/ppermute | solution.py:27
  204.1 336.2 %reduce-scatter.2.cloned.1.call-start = ((), (), s32[]{:S(2)}) async-start(), calls=%async_computation.4 | async-start | bytes 10027008 | tf_op jit(solution)/shard_map/reduce_scatter | solution.py:665
  222.0 2.9 collective-permute-start.9
  282.3 21.2 %copy-start.11 = (bf16[1,512,1024]{2,1,0:T(8,128)(2,1)S(1)}, bf16[1,512,1024]{2,1,0:T(8,128)(2,1)}, u32[]{:S(2)}) copy-start(bf16[1,512,1024]{2,1,0:T(8,128)(2,1)} %param.19) | copy-start | bytes 3145732
  282.5 21.0 %collective-permute-start.10 = (bf16[512,1024]{1,0:T(8,128)(2,1)S(1)}, bf16[512,1024]{1,0:T(8,128)(2,1)S(1)}, u32[]{:S(2)}, u32[]{:S(2)}) collective-permute-start(bf16[512,1024]{1,0:T(8,128)(2,1)S(1)} %dynamic-slice_convert_fusion.3), channel_id=1, source_target_pairs={{0,2},{2,0},{1,3},{3,1},{4,6},{6,4},{5,7},{7,5},{8,10},{10,8},{9,1... | collective-permute-start | bytes 3145736 | tf_op jit(solution)/shard_map/ppermute | solution.py:27
  284.3 1.2 collective-permute-start.11
  286.2 3.7 collective-permute-start.12
  290.5 3.7 collective-permute-start.13
  294.2 4.5 collective-permute-start.14
  298.7 3.6 collective-permute-start.15
  306.6 2.7 collective-permute-start.16
  332.1 16.0 %collective-permute-start.17 = (bf16[512,1024]{1,0:T(8,128)(2,1)}, bf16[512,1024]{1,0:T(8,128)(2,1)}, u32[]{:S(2)}, u32[]{:S(2)}) collective-permute-start(bf16[512,1024]{1,0:T(8,128)(2,1)} %dynamic-slice_convert_fusion.2), channel_id=1, source_target_pairs={{0,2},{2,0},{1,3},{3,1},{4,6},{6,4},{5,7},{7,5},{8,10},{10,8},{9,1... | collective-permute-start | bytes 3145736 | tf_op jit(solution)/shard_map/ppermute | solution.py:27
  356.0 6.8 collective-permute-start.18
  369.1 174.0 %copy-start.34 = (bf16[512,1024]{1,0:T(8,128)(2,1)S(1)}, bf16[512,1024]{1,0:T(8,128)(2,1)}, u32[]{:S(2)}) copy-start(bf16[512,1024]{1,0:T(8,128)(2,1)} %copy-done.33) | copy-start | bytes 3145732
  369.1 173.9 %copy-start.74 = (bf16[512,1024]{1,0:T(8,128)(2,1)S(1)}, bf16[512,1024]{1,0:T(8,128)(2,1)}, u32[]{:S(2)}) copy-start(bf16[512,1024]{1,0:T(8,128)(2,1)} %all-gather.5.cloned.1.call-done) | copy-start | bytes 3145732
  369.1 526.3 %all-gather.11.cloned.1.call-start = ((), (), s32[]{:S(2)}) async-start(), calls=%async_computation.5 | async-start | bytes 10027008 | tf_op jit(solution)/shard_map/all_gather | solution.py:666
  544.5 18.8 %collective-permute-start.19 = (bf16[1024,256]{1,0:T(8,128)(2,1)S(1)}, bf16[1024,256]{1,0:T(8,128)(2,1)S(1)}, u32[]{:S(2)}, u32[]{:S(2)}) collective-permute-start(bf16[1024,256]{1,0:T(8,128)(2,1)S(1)} %get-tuple-element.102), channel_id=1, source_target_pairs={{0,4},{4,0},{1,5},{5,1},{2,6},{6,2},{3,7},{7,3},{8,12},{12,8},{9,1... | collective-permute-start | bytes 1572872 | tf_op jit(solution)/shard_map/ppermute | solution.py:27
  588.2 117.4 %collective-permute-start.21 = (bf16[2048,512]{1,0:T(8,128)(2,1)}, bf16[2048,512]{1,0:T(8,128)(2,1)S(1)}, u32[]{:S(2)}, u32[]{:S(2)}) collective-permute-start(bf16[2048,512]{1,0:T(8,128)(2,1)} %get-tuple-element.34), channel_id=1, source_target_pairs={{0,8},{8,16},{16,24},{1,9},{9,17},{17,25},{2,10},{10,18},{18,26},{... | collective-permute-start | bytes 6291464 | tf_op jit(solution)/shard_map/ppermute | solution.py:716
  601.7 103.9 %collective-permute-start.20 = (bf16[2048,512]{1,0:T(8,128)(2,1)}, bf16[2048,512]{1,0:T(8,128)(2,1)}, u32[]{:S(2)}, u32[]{:S(2)}) collective-permute-start(bf16[2048,512]{1,0:T(8,128)(2,1)} %get-tuple-element.33), channel_id=1, source_target_pairs={{8,0},{16,8},{24,16},{9,1},{17,9},{25,17},{10,2},{18,10},{26,18},{... | collective-permute-start | bytes 6291464 | tf_op jit(solution)/shard_map/ppermute | solution.py:714
  732.2 42.9 %collective-permute-start.22 = (bf16[1024,1024]{1,0:T(8,128)(2,1)}, bf16[1024,1024]{1,0:T(8,128)(2,1)}, u32[]{:S(2)}, u32[]{:S(2)}) collective-permute-start(bf16[1024,1024]{1,0:T(8,128)(2,1)} %dynamic-slice_convert_fusion), channel_id=1, source_target_pairs={{0,4},{4,0},{1,5},{5,1},{2,6},{6,2},{3,7},{7,3},{8,12},{12,8},{9,1... | collective-permute-start | bytes 6291464 | tf_op jit(solution)/shard_map/ppermute | solution.py:27
  740.0 13.7 %collective-permute-start.29 = (bf16[512,768]{0,1:T(8,128)(2,1)S(1)}, bf16[512,768]{0,1:T(8,128)(2,1)S(1)}, u32[]{:S(2)}, u32[]{:S(2)}) collective-permute-start(bf16[512,768]{0,1:T(8,128)(2,1)S(1)} %dynamic-slice_convert_fusion.5), channel_id=1, source_target_pairs={{0,1},{1,0},{2,3},{3,2},{4,5},{5,4},{6,7},{7,6},{8,9},{9,8},{10,11... | collective-permute-start | bytes 2359304 | tf_op jit(solution)/shard_map/ppermute | solution.py:56
  755.4 9.9 %collective-permute-start.30 = (bf16[256,768]{0,1:T(8,128)(2,1)S(1)}, bf16[256,768]{0,1:T(8,128)(2,1)S(1)}, u32[]{:S(2)}, u32[]{:S(2)}) collective-permute-start(bf16[256,768]{0,1:T(8,128)(2,1)S(1)} %dynamic-slice_convert_fusion.6), channel_id=1, source_target_pairs={{0,8},{8,0},{16,24},{24,16},{1,9},{9,1},{17,25},{25,17},{2,10},{10... | collective-permute-start | bytes 1179656 | tf_op jit(solution)/shard_map/ppermute | solution.py:56
  765.5 16.2 %collective-permute-start.31 = (bf16[128,768]{0,1:T(8,128)(2,1)S(1)}, bf16[128,768]{0,1:T(8,128)(2,1)S(1)}, u32[]{:S(2)}, u32[]{:S(2)}) collective-permute-start(bf16[128,768]{0,1:T(8,128)(2,1)S(1)} %dynamic-slice_convert_fusion.7), channel_id=1, source_target_pairs={{0,16},{8,24},{16,0},{24,8},{1,17},{9,25},{17,1},{25,9},{2,18},{10... | collective-permute-start | bytes 589832 | tf_op jit(solution)/shard_map/ppermute | solution.py:56
  781.7 20.3 %collective-permute-start.23 = (bf16[512,1024]{1,0:T(8,128)(2,1)}, bf16[512,1024]{1,0:T(8,128)(2,1)}, u32[]{:S(2)}, u32[]{:S(2)}) collective-permute-start(bf16[512,1024]{1,0:T(8,128)(2,1)} %dynamic-slice_convert_fusion.1), channel_id=1, source_target_pairs={{0,2},{2,0},{1,3},{3,1},{4,6},{6,4},{5,7},{7,5},{8,10},{10,8},{9,1... | collective-permute-start | bytes 3145736 | tf_op jit(solution)/shard_map/ppermute | solution.py:27
  781.7 8.3 collective-permute-start.32
  790.1 10.8 %collective-permute-start.33 = (bf16[256,768]{0,1:T(8,128)(2,1)S(1)}, bf16[256,768]{0,1:T(8,128)(2,1)S(1)}, u32[]{:S(2)}, u32[]{:S(2)}) collective-permute-start(bf16[256,768]{0,1:T(8,128)(2,1)S(1)} %maximum_select_fusion.23), channel_id=1, source_target_pairs={{0,8},{8,0},{16,24},{24,16},{1,9},{9,1},{17,25},{25,17},{2,10},{10... | collective-permute-start | bytes 1179656 | tf_op jit(solution)/shard_map/ppermute | solution.py:65
  802.0 16.6 %collective-permute-start.34 = (bf16[1,512,768]{1,2,0:T(8,128)(2,1)}, bf16[1,512,768]{1,2,0:T(8,128)(2,1)}, u32[]{:S(2)}, u32[]{:S(2)}) collective-permute-start(bf16[1,512,768]{1,2,0:T(8,128)(2,1)} %maximum_select_fusion.17), channel_id=1, source_target_pairs={{0,2},{2,0},{1,3},{3,1},{4,6},{6,4},{5,7},{7,5},{8,10},{10,8},{9,1... | collective-permute-start | bytes 2359304 | tf_op jit(solution)/shard_map/ppermute | solution.py:65
  810.7 7.4 collective-permute-start.24
  818.1 11.4 %collective-permute-start.25 = (f32[48,1024]{1,0:T(8,128)S(1)}, f32[48,1024]{1,0:T(8,128)S(1)}, u32[]{:S(2)}, u32[]{:S(2)}) collective-permute-start(f32[48,1024]{1,0:T(8,128)S(1)} %pad_add_fusion.5), channel_id=1, source_target_pairs={{0,16},{8,24},{16,0},{24,8},{1,17},{9,25},{17,1},{25,9},{2,18},{10... | collective-permute-start | bytes 589832 | tf_op jit(solution)/shard_map/ppermute | solution.py:73
  820.8 55.8 %collective-permute-start.35 = (bf16[2,512,768]{1,2,0:T(8,128)(2,1)S(1)}, bf16[2,512,768]{1,2,0:T(8,128)(2,1)S(1)}, u32[]{:S(2)}, u32[]{:S(2)}) collective-permute-start(bf16[2,512,768]{1,2,0:T(8,128)(2,1)S(1)} %maximum_select_fusion.13), channel_id=1, source_target_pairs={{0,4},{4,0},{1,5},{5,1},{2,6},{6,2},{3,7},{7,3},{8,12},{12,8},{9,1... | collective-permute-start | bytes 4718600 | tf_op jit(solution)/shard_map/ppermute | solution.py:65
  822.6 38.3 %copy-start.61 = (f32[512]{0:T(512)S(1)}, f32[512]{0:T(512)}, u32[]{:S(2)}) copy-start(f32[512]{0:T(512)} %get-tuple-element.37) | copy-start | bytes 6148
  822.6 39.9 %copy-start.13 = (f32[512,1024]{1,0:T(8,128)S(1)}, f32[512,1024]{1,0:T(8,128)}, u32[]{:S(2)}) copy-start(f32[512,1024]{1,0:T(8,128)} %get-tuple-element.68) | copy-start | bytes 6291460
  822.6 39.9 %copy-start.14 = (f32[512,1024]{1,0:T(8,128)S(1)}, f32[512,1024]{1,0:T(8,128)}, u32[]{:S(2)}) copy-start(f32[512,1024]{1,0:T(8,128)} %get-tuple-element.60) | copy-start | bytes 6291460
  822.6 39.9 %copy-start.50 = (f32[512]{0:T(512)S(1)}, f32[512]{0:T(512)}, u32[]{:S(2)}) copy-start(f32[512]{0:T(512)} %copy-done.48) | copy-start | bytes 6148
  829.6 31.3 %collective-permute-start.26 = (f32[48,1024]{1,0:T(8,128)S(1)}, f32[48,1024]{1,0:T(8,128)S(1)}, u32[]{:S(2)}, u32[]{:S(2)}) collective-permute-start(f32[48,1024]{1,0:T(8,128)S(1)} %add.1172), channel_id=1, source_target_pairs={{0,4},{4,0},{1,5},{5,1},{2,6},{6,2},{3,7},{7,3},{8,12},{12,8},{9,1... | collective-permute-start | bytes 589832 | tf_op jit(solution)/shard_map/ppermute | solution.py:73
  860.9 1.5 collective-permute-start.27
  862.4 7.0 collective-permute-start.28
  (77 other events, 436.1 us)
Sparse Core Ops, SparseCore 0:
  10.2 23.9 all-gather.4
  46.8 56.6 all-gather.6
  204.2 70.5 all-gather.8
  369.2 171.0 reduce-scatter.1
  542.7 93.2 all-gather.10
